TPU v7x, 128 devices: a whole 4x4x4 slice. The times are simulated.
128 devices in a mesh: wall: 4 (over x), drops: 32 (over y, z, core).
Axes of the slice: x: 4, y: 4, z: 4, core: 2. Of those that a mesh axis runs over, the one named last changes fastest.
Arguments:
- drop_points: float32 [1024, 3, 544], P(('wall', 'drops')), may hold values from -6 to 6
- drop_strength: float32 [1024, 3, 544], P(('wall', 'drops')), may hold values from -0.25 to 0.25
- upsample: float32 [544, 2112], replicated, may hold values from -0.25 to 0.25
- base_velocity: float32 [1024, 3, 544], P(('wall', 'drops')), may hold values from -6 to 6
- near_drops: int32 [1024, 4], P(('wall', 'drops')), may hold values from 0 to 1023, as said below
- near_count: int32 [1024], P(('wall', 'drops')), may hold values from 2 to 4
- patch_points: float32 [8192, 192], P('wall'), may hold values from -6 to 6
- patch_strength: float32 [8192, 192], P('wall'), may hold values from -1 to 1
- wall_near: int32 [1024, 8], P(('wall', 'drops')), may hold values from 0 to 8191
Outputs:
- drop_velocity: float32 [1024, 3, 544], P(('wall', 'drops'))
Inputs may be any that keep to these rules, and one draw needn't show every extreme that they name: `near_drops`: each entry names a drop of the same drop group (same index along wall). Of the 32 entries of one device, at most 2 name drops of any one device of the group, and on every device some device of the group is named exactly 2 times. Entries at slots k >= near_count are ignored.
All inputs are finite; a program needn't handle non-finite values.
Results may differ from a plain program's by a relative error of at most 0.0003.
Values sent between devices are 32-bit elements; how exact they have to be, the bound alone decides.
No kernel may reach another device: no remote copies, remote signals or barrier semaphores. Data moves between devices by JAX's collectives and lax.ppermute only.
A program may use at most 128 MiB of HBM per device.

v0:
```python
import jax
import jax.numpy as jnp
from jax import lax
from jax.experimental import pallas as pl
from jax.experimental.pallas import tpu as pltpu
from jax.sharding import PartitionSpec as P


smoothing_square = 0.25
f32 = jnp.float32
bf16 = jnp.bfloat16


def nn(a, b):
    return jnp.dot(a, b, preferred_element_type=f32)


def split(v, count):
    out = []
    for left in reversed(range(count)):
        p = v.astype(bf16)
        out.append(p)
        if left:
            v = v - p.astype(f32)
    return out


def source_rows(row):
    y = [row(c) for c in range(3)]
    g = [row(3 + c) for c in range(3)]
    width = y[0].shape[1]
    y = [jnp.broadcast_to(v, (8, width)) for v in y]
    g = [jnp.broadcast_to(v, (8, width)) for v in g]
    at = lax.broadcasted_iota(jnp.int32, (8, width), 0)

    def lay(*values):
        out = values[-1]
        for r in range(len(values) - 2, -1, -1):
            if values[r] is not values[r + 1]:
                out = jnp.where(at <= r, values[r], out)
        return out

    one = jnp.ones((8, width), f32)
    zero = jnp.zeros((8, width), f32)
    square = y[0] * y[0] + y[1] * y[1] + y[2] * y[2]
    along = y[0] * g[0] + y[1] * g[1] + y[2] * g[2]
    grown = square + 2.0 * smoothing_square
    top = lay(g[0], g[1], g[2], g[0], g[1], g[2], g[0], g[1]) * lay(
        one, one, one, y[0], y[0], y[0], y[1], y[1]
    )
    low = lay(g[2], g[0], g[1], g[2], g[0], g[1], g[2], g[2]) * lay(
        y[1], y[2], y[2], y[2], grown, grown, grown, zero
    ) + along * lay(zero, zero, zero, zero, y[0], y[1], y[2], zero)
    c = split(jnp.concatenate([top, low], axis=0), 3)
    b = [p.astype(f32) for p in split(lay(y[0], y[1], y[2], square, y[0], y[1], y[2], square), 3)]
    first = jnp.where(at < 4, b[0], b[1])
    second = jnp.where(at < 4, b[2], one)
    dist = jnp.concatenate([first, second, first, b[0]], axis=0).astype(bf16)
    return dist, jnp.concatenate(c, axis=0), jnp.concatenate(c[:2], axis=0)


def target_rows(x):
    square = x[0] * x[0] + x[1] * x[1] + x[2] * x[2] + smoothing_square
    one = jnp.ones_like(square)
    zero = jnp.zeros_like(square)
    a = [split(-2.0 * v, 3) for v in x]
    a = [[p.astype(f32) for p in v] for v in a]
    s = [p.astype(f32) for p in split(square, 3)]
    top = [a[0][0], a[1][0], a[2][0], one]
    rows = top * 3 + s + [zero]
    rows += [a[0][1], a[1][1], a[2][1], zero] * 2
    rows += [a[0][2], a[1][2], a[2][2], zero] + [zero] * 4
    return jnp.concatenate(rows, axis=0).astype(bf16)


def accumulate(acc_ref, xf, row):
    dist_rows, three, two = source_rows(row)
    dist = lax.dot_general(dist_rows, xf, (((0,), (0,)), ((), ())), preferred_element_type=f32)
    w = lax.rsqrt(dist)
    w3 = w * w * w
    hi = w3.astype(bf16)
    lo = (w3 - hi.astype(f32)).astype(bf16)
    acc_ref[:48] += nn(three, hi)
    acc_ref[48:] += nn(two, lo)


def finish(acc_ref, t_ref, b_ref, o_ref, drop):
    q = acc_ref[0:16] + acc_ref[16:32] + acc_ref[32:48] + (acc_ref[48:64] + acc_ref[64:80])
    at = pl.ds(drop, 1)
    x = [t_ref[i, at] for i in range(3)]
    square = x[0] * x[0] + x[1] * x[1] + x[2] * x[2]
    gs = [q[a : a + 1] for a in range(3)]
    h = [[q[3 + 3 * b + a : 4 + 3 * b + a] for a in range(3)] for b in range(3)]
    m = [q[12 + a : 13 + a] for a in range(3)]
    lean = x[0] * gs[0] + x[1] * gs[1] + x[2] * gs[2] - (h[0][0] + h[1][1] + h[2][2])
    for a in range(3):
        u = m[a] + square * gs[a] + x[a] * lean
        for b in range(3):
            u = u - x[b] * (2.0 * h[b][a] + h[a][b])
        o_ref[a, at] = b_ref[a, at] + u


def wall_kernel(wall_ref, t_ref, b_ref, o_ref, acc_ref):
    drop = pl.program_id(0)
    acc_ref[...] = jnp.zeros_like(acc_ref)
    xf = target_rows([t_ref[i, pl.ds(drop, 1)] for i in range(3)])
    accumulate(acc_ref, xf, lambda c: wall_ref[drop, c : c + 1])
    finish(acc_ref, t_ref, b_ref, o_ref, drop)


def near_kernel(
    count_ref, pick_ref, got_ref, up_ref, t_ref, b_ref, o_ref,
    cbuf, f_ref, acc_ref, xf_ref,
):
    drop = pl.program_id(0)
    slot = pl.program_id(1)
    slots = pl.num_programs(1)
    entries = f_ref.shape[0]
    depth = got_ref.shape[2]
    coarse = got_ref.shape[3]
    fine = up_ref.shape[1]

    @pl.when((drop == 0) & (slot == 0))
    def _():
        pad = jnp.zeros((2, coarse), f32)
        for e in range(entries):
            both = got_ref[pick_ref[e] // depth]
            place = pick_ref[e] % depth
            row = both[:, 0]
            for p in range(1, depth):
                row = jnp.where(place == p, both[:, p], row)
            cbuf[e] = jnp.concatenate([row, pad], axis=0)
        source = cbuf[...]
        high, low = split(source.reshape(entries * 8, coarse), 2)
        step = 384
        for u0 in range(0, fine, step):
            u1 = min(fine, u0 + step)
            up = split(up_ref[:, u0:u1], 2)
            f = nn(high, up[0]) + (nn(low, up[0]) + nn(high, up[1]))
            f_ref[:, :, u0:u1] = f.reshape(entries, 8, u1 - u0)
        tail = f_ref.shape[2] - fine - coarse
        at = lax.broadcasted_iota(jnp.int32, source.shape, 1)
        source = jnp.where(at < 3, source, -source)
        f_ref[:, :, fine:] = jnp.concatenate(
            [source, jnp.zeros((entries, 8, tail), f32)], axis=2
        )

    @pl.when(slot == 0)
    def _():
        xf_ref[...] = target_rows([t_ref[i, pl.ds(drop, 1)] for i in range(3)])
        acc_ref[...] = jnp.zeros_like(acc_ref)

    @pl.when(slot < count_ref[drop])
    def _():
        accumulate(acc_ref, xf_ref[...], lambda c: f_ref[drop * slots + slot, c : c + 1])

    @pl.when(slot == slots - 1)
    def _():
        finish(acc_ref, t_ref, b_ref, o_ref, drop)


def whole(a):
    zeros = (0,) * len(a.shape)
    return pl.BlockSpec(a.shape, lambda *_: zeros, pipeline_mode=pl.Buffered(1))


def wall_sums(wall, targets, base):
    _, owned, nodes = targets.shape
    return pl.pallas_call(
        wall_kernel,
        grid=(owned,),
        in_specs=[whole(wall), whole(targets), whole(base)],
        out_specs=whole(targets),
        scratch_shapes=[
            pltpu.VMEM((80, nodes), f32),
        ],
        out_shape=jax.ShapeDtypeStruct(targets.shape, f32),
        name="wall_pairs",
    )(wall, targets, base)


def near_sums(counts, pick, got, upsample, targets, base):
    _, owned, nodes = targets.shape
    entries = pick.shape[0]
    slots = entries // owned
    width = -(-(upsample.shape[1] + nodes) // 128) * 128
    return pl.pallas_call(
        near_kernel,
        grid_spec=pltpu.PrefetchScalarGridSpec(
            num_scalar_prefetch=2,
            grid=(owned, slots),
            in_specs=[whole(got), whole(upsample), whole(targets), whole(base)],
            out_specs=whole(targets),
            scratch_shapes=[
                pltpu.VMEM((entries, 8, nodes), f32),
                pltpu.VMEM((entries, 8, width), f32),
                pltpu.VMEM((80, nodes), f32),
                pltpu.VMEM((32, nodes), bf16),
            ],
        ),
        out_shape=jax.ShapeDtypeStruct(targets.shape, f32),
        name="near_pairs",
    )(counts, pick, got, upsample, targets, base)


def per_device(
    drop_points,
    drop_strength,
    upsample,
    base_velocity,
    near_drops,
    near_count,
    patch_points,
    patch_strength,
    wall_near,
):
    ranks = lax.axis_size("drops")
    walls = lax.axis_size("wall")
    owned, _, coarse = drop_points.shape
    slots = near_drops.shape[1]
    entries = owned * slots
    depth = max(2, (entries + ranks - 1) // ranks)
    here = lax.axis_index("wall")

    partner = near_drops.reshape(entries)
    owner = partner // owned % ranks
    local = partner % owned
    member = (owner[:, None] == jnp.arange(ranks, dtype=jnp.int32)[None, :]).astype(jnp.int32)
    position = jnp.sum((jnp.cumsum(member, axis=0) - 1) * member, axis=1)
    slot_hit = member[:, :, None] * (
        position[:, None, None] == jnp.arange(depth, dtype=jnp.int32)[None, None, :]
    ).astype(jnp.int32)
    requests = jnp.sum(slot_hit * local[:, None, None], axis=0)
    incoming = lax.all_to_all(requests, "drops", split_axis=0, concat_axis=0, tiled=True)

    both = jnp.concatenate([drop_points, drop_strength], axis=1)
    send = jnp.take(both, incoming.reshape(ranks * depth), axis=0)
    send = send.reshape(ranks, depth, 6, coarse).transpose(0, 2, 1, 3)

    held = patch_points.shape[0]
    listed = wall_near.shape[1]
    wanted, send = lax.optimization_barrier((wall_near.reshape(owned * listed), send))
    got = lax.all_to_all(send, "drops", split_axis=0, concat_axis=0, tiled=True)
    asked = [wanted]
    for r in range(1, walls):
        asked.append(lax.ppermute(wanted, "wall", [(w, (w + r) % walls) for w in range(walls)]))

    index = jnp.clip(jnp.concatenate(asked) - here * held, 0, held - 1)
    rows = jnp.concatenate(
        [jnp.take(patch_points, index, axis=0), jnp.take(patch_strength, index, axis=0)], axis=1
    )
    rows = rows.reshape(walls, owned * listed, -1)
    home = wanted // held
    mine = rows[0]
    for r in range(1, walls):
        back = lax.ppermute(rows[r], "wall", [(w, (w - r) % walls) for w in range(walls)])
        mine = jnp.where((home == (here + r) % walls)[:, None], back, mine)
    patch = rows.shape[2] // 6
    mine = mine.reshape(owned, listed, 6, patch).transpose(0, 2, 1, 3).reshape(owned, 6, -1)

    targets = drop_points.transpose(1, 0, 2)
    total = near_sums(
        near_count, owner * depth + position, got, upsample, targets, base_velocity.transpose(1, 0, 2)
    )
    total = wall_sums(mine, targets, total)
    return total.transpose(1, 0, 2)


def solution(mesh):
    return jax.shard_map(
        per_device,
        mesh=mesh,
        in_specs=(
            P(("wall", "drops"), None, None),
            P(("wall", "drops"), None, None),
            P(),
            P(("wall", "drops"), None, None),
            P(("wall", "drops"), None),
            P(("wall", "drops")),
            P("wall", None),
            P("wall", None),
            P(("wall", "drops"), None),
        ),
        out_specs=P(("wall", "drops"), None, None),
        check_vma=False,
    )
```

profile of v0, /device:TPU:113, one launch (start us, length us, event | category | flops | bytes accessed | tf_op | source)
XLA Modules:
  0.0 142.8 jit_solution(15425539056311317854)
XLA Ops:
  0.0 0.8 copy.39
  2.0 7.4 %all-to-all-start = ((s32[32,1,2]{2,1,0:T(1,128)}), s32[32,1,2]{2,1,0:T(1,128)S(1)}, u32[]{:S(2)}, u32[]{:S(2)}) async-start(s32[32,1,2]{2,1,0:T(1,128)} %copy.40), calls=%async_computation | async-start | bytes 32768 | tf_op jit(solution)/shard_map/all_to_all | solution.py:234
  10.0 0.8 reshape.180
  10.7 0.9 copy.44
  11.6 0.9 copy.43
  12.4 2.8 %copy.47 = f32[2048,192]{1,0:T(8,128)} copy(f32[2048,192]{0,1:T(8,128)} %param.17) | data formatting | bytes 3145728 | tf_op args[6]
  15.3 1.8 %copy.48 = f32[2048,192]{1,0:T(8,128)S(1)} copy(f32[2048,192]{0,1:T(8,128)} %param.18) | data formatting | bytes 3145728 | tf_op args[7]
  18.7 1.7 %gather_fusion = f32[64,6,544]{2,1,0:T(8,128)} fusion(f32[8,6,544]{2,1,0:T(8,128)S(1)} %pad_maximum_fusion, s32[1024]{0:T(1024)S(1)} %pad_clamp_fusion.1), kind=kCustom, calls=%fused_computation.2 | custom fusion | bytes 1671424 | tf_op jit(solution)/shard_map/jit(_take)/gather | solution.py:237
  20.4 2.9 %fusion = f32[32,6,2,544]{3,2,1,0:T(2,128)} fusion(f32[32,2,6,544]{3,2,1,0:T(8,128)} %bitcast.14, pred[32,2]{1,0:T(8,128)(4,1)S(1)} %copy.42), kind=kLoop, calls=%fused_computation.4 | loop fusion | flops 208896 | bytes 1671232 | tf_op jit(solution)/shard_map/transpose | solution.py:238
  23.4 1.2 collective-permute-start
  24.6 1.5 %collective-permute-start.2 = (s32[64]{0:T(128)S(1)}, s32[64]{0:T(128)S(1)}, u32[]{:S(2)}, u32[]{:S(2)}) collective-permute-start(s32[64]{0:T(128)S(1)} %reshape.180), channel_id=1, source_target_pairs={{0,96},{32,0},{64,32},{96,64},{1,97},{33,1},{65,33},{97,65},{2,98}... | collective-permute-start | bytes 776 | tf_op jit(solution)/shard_map/ppermute | solution.py:246
  26.0 1.5 %collective-permute-start.1 = (s32[64]{0:T(128)S(1)}, s32[64]{0:T(128)S(1)}, u32[]{:S(2)}, u32[]{:S(2)}) collective-permute-start(s32[64]{0:T(128)S(1)} %reshape.180), channel_id=1, source_target_pairs={{0,64},{32,96},{64,0},{96,32},{1,65},{33,97},{65,1},{97,33},{2,66}... | collective-permute-start | bytes 776 | tf_op jit(solution)/shard_map/ppermute | solution.py:246
  27.6 8.2 %all-to-all-start.1 = ((f32[32,6,2,544]{3,2,1,0:T(2,128)}), f32[32,6,2,544]{3,2,1,0:T(2,128)S(1)}, u32[]{:S(2)}, u32[]{:S(2)}) async-start(f32[32,6,2,544]{3,2,1,0:T(2,128)} %fusion), calls=%async_computation.1 | async-start | bytes 1966080 | tf_op jit(solution)/shard_map/all_to_all | solution.py:243
  36.0 2.6 %gather_fusion.1 = f32[256,192]{1,0:T(8,128)S(1)} fusion(f32[2048,192]{1,0:T(8,128)} %copy.47, s32[1024]{0:T(1024)S(1)} %pad_clamp_fusion), kind=kCustom, calls=%fused_computation.clone | custom fusion | bytes 394240 | tf_op jit(solution)/shard_map/jit(_take)/gather | solution.py:250
  38.5 1.7 %gather_fusion.2 = f32[256,192]{1,0:T(8,128)} fusion(f32[2048,192]{1,0:T(8,128)S(1)} %copy.48, s32[1024]{0:T(1024)S(1)} %pad_clamp_fusion), kind=kCustom, calls=%fused_computation.1.clone | custom fusion | bytes 394240 | tf_op jit(solution)/shard_map/jit(_take)/gather | solution.py:250
  40.2 1.1 broadcast_select_fusion
  41.4 0.9 collective-permute-start.5
  42.9 1.4 %collective-permute-start.4 = (f32[64,384]{1,0:T(8,128)S(1)}, f32[64,384]{1,0:T(8,128)S(1)}, u32[]{:S(2)}, u32[]{:S(2)}) collective-permute-start(f32[64,384]{1,0:T(8,128)S(1)} %get-tuple-element.16), channel_id=1, source_target_pairs={{0,64},{32,96},{64,0},{96,32},{1,65},{33,97},{65,1},{97,33},{2,66}... | collective-permute-start | bytes 294920 | tf_op jit(solution)/shard_map/ppermute | solution.py:256
  44.3 1.1 collective-permute-done.5
  45.4 2.1 %collective-permute-done.3 = f32[64,384]{1,0:T(8,128)S(1)} collective-permute-done((f32[64,384]{1,0:T(8,128)S(1)}, f32[64,384]{1,0:T(8,128)S(1)}, u32[]{:S(2)}, u32[]{:S(2)}) %collective-permute-start.3) | collective-permute-done | bytes 98336 | tf_op jit(solution)/shard_map/ppermute | solution.py:256
  47.5 1.6 %collective-permute-done.4 = f32[64,384]{1,0:T(8,128)S(1)} collective-permute-done((f32[64,384]{1,0:T(8,128)S(1)}, f32[64,384]{1,0:T(8,128)S(1)}, u32[]{:S(2)}, u32[]{:S(2)}) %collective-permute-start.4) | collective-permute-done | bytes 98336 | tf_op jit(solution)/shard_map/ppermute | solution.py:256
  50.1 1.0 copy-done
  51.1 84.1 %near_pairs.1.b_ref = f32[3,8,544]{2,1,0:T(8,128)} custom-call(s32[8]{0:T(128)} %count_ref.1, s32[32]{0:T(128)} %multiply_add_fusion.pick_ref, f32[32,6,2,544]{3,2,1,0:T(2,128)} %copy-done, f32[544,2112]{1,0:T(8,128)} %up_ref.1, f32[3,8,544]{2,1,0:T(8,128)} %bitcast.16, f32[3,8,544]{2,1,0:T(8,128)} %bitcast.18), custom_call_target="tpu_custom_call" | custom-call | tf_op jit(solution)/shard_map/near_pairs/pallas_call | solution.py:187
  135.2 7.6 %wall_pairs.1 = f32[3,8,544]{2,1,0:T(8,128)} custom-call(f32[8,6,512]{2,1,0:T(8,128)} %reshape.216.wall_ref, f32[3,8,544]{2,1,0:T(8,128)} %bitcast.17, f32[3,8,544]{2,1,0:T(8,128)} %near_pairs.1.b_ref), custom_call_target="tpu_custom_call" | custom-call | tf_op jit(solution)/shard_map/wall_pairs/pallas_call | solution.py:169
  (34 shorter events, 5.2 us)
Async XLA Ops:
  2.0 15.2 %all-to-all-start = ((s32[32,1,2]{2,1,0:T(1,128)}), s32[32,1,2]{2,1,0:T(1,128)S(1)}, u32[]{:S(2)}, u32[]{:S(2)}) async-start(s32[32,1,2]{2,1,0:T(1,128)} %copy.40), calls=%async_computation | async-start | bytes 32768 | tf_op jit(solution)/shard_map/all_to_all | solution.py:234
  23.4 12.5 %collective-permute-start = (s32[64]{0:T(128)S(1)}, s32[64]{0:T(128)S(1)}, u32[]{:S(2)}, u32[]{:S(2)}) collective-permute-start(s32[64]{0:T(128)S(1)} %reshape.180), channel_id=1, source_target_pairs={{0,32},{32,64},{64,96},{96,0},{1,33},{33,65},{65,97},{97,1},{2,34}... | collective-permute-start | bytes 776 | tf_op jit(solution)/shard_map/ppermute | solution.py:246
  24.6 11.3 %collective-permute-start.2 = (s32[64]{0:T(128)S(1)}, s32[64]{0:T(128)S(1)}, u32[]{:S(2)}, u32[]{:S(2)}) collective-permute-start(s32[64]{0:T(128)S(1)} %reshape.180), channel_id=1, source_target_pairs={{0,96},{32,0},{64,32},{96,64},{1,97},{33,1},{65,33},{97,65},{2,98}... | collective-permute-start | bytes 776 | tf_op jit(solution)/shard_map/ppermute | solution.py:246
  26.0 9.8 %collective-permute-start.1 = (s32[64]{0:T(128)S(1)}, s32[64]{0:T(128)S(1)}, u32[]{:S(2)}, u32[]{:S(2)}) collective-permute-start(s32[64]{0:T(128)S(1)} %reshape.180), channel_id=1, source_target_pairs={{0,64},{32,96},{64,0},{96,32},{1,65},{33,97},{65,1},{97,33},{2,66}... | collective-permute-start | bytes 776 | tf_op jit(solution)/shard_map/ppermute | solution.py:246
  27.6 22.5 %all-to-all-start.1 = ((f32[32,6,2,544]{3,2,1,0:T(2,128)}), f32[32,6,2,544]{3,2,1,0:T(2,128)S(1)}, u32[]{:S(2)}, u32[]{:S(2)}) async-start(f32[32,6,2,544]{3,2,1,0:T(2,128)} %fusion), calls=%async_computation.1 | async-start | bytes 1966080 | tf_op jit(solution)/shard_map/all_to_all | solution.py:243
  41.4 4.0 %collective-permute-start.5 = (f32[64,384]{1,0:T(8,128)S(1)}, f32[64,384]{1,0:T(8,128)S(1)}, u32[]{:S(2)}, u32[]{:S(2)}) collective-permute-start(f32[64,384]{1,0:T(8,128)S(1)} %get-tuple-element.14), channel_id=1, source_target_pairs={{0,96},{32,0},{64,32},{96,64},{1,97},{33,1},{65,33},{97,65},{2,98}... | collective-permute-start | bytes 294920 | tf_op jit(solution)/shard_map/ppermute | solution.py:256
  42.3 5.2 %collective-permute-start.3 = (f32[64,384]{1,0:T(8,128)S(1)}, f32[64,384]{1,0:T(8,128)S(1)}, u32[]{:S(2)}, u32[]{:S(2)}) collective-permute-start(f32[64,384]{1,0:T(8,128)S(1)} %get-tuple-element.15), channel_id=1, source_target_pairs={{0,32},{32,64},{64,96},{96,0},{1,33},{33,65},{65,97},{97,1},{2,34}... | collective-permute-start | bytes 294920 | tf_op jit(solution)/shard_map/ppermute | solution.py:256
  42.9 6.2 %collective-permute-start.4 = (f32[64,384]{1,0:T(8,128)S(1)}, f32[64,384]{1,0:T(8,128)S(1)}, u32[]{:S(2)}, u32[]{:S(2)}) collective-permute-start(f32[64,384]{1,0:T(8,128)S(1)} %get-tuple-element.16), channel_id=1, source_target_pairs={{0,64},{32,96},{64,0},{96,32},{1,65},{33,97},{65,1},{97,33},{2,66}... | collective-permute-start | bytes 294920 | tf_op jit(solution)/shard_map/ppermute | solution.py:256
  50.1 1.0 copy-start
where the time goes:
time: 143 us
  Pallas kernels  91.7 us (64%)
  starting transfers between devices  22.8 us (16%)
  local copies, waits for them, and re-layouts  17.2 us (12%)
  other arithmetic  6.05 us (4%)
  waiting for transfers between devices  4.77 us (3%)
    pallas_call x1, Pallas kernels, near_sums(): pl.pallas_call(near_kernel, grid_spec=pltpu.PrefetchScalarGridSpec(num_sc...  84.1 us
    all_to_all x1, starting transfers between devices, per_device(): got = lax.all_to_all(send, 'drops', split_axis=0, concat_axis=0, tiled=True)  8.23 us
    unnamed x7, local copies, waits for them, and re-layouts  8.1 us
    pallas_call x1, Pallas kernels, wall_sums(): pl.pallas_call(wall_kernel, grid=(owned,), in_specs=[whole(wall), whole(t...  7.55 us
    all_to_all x1, starting transfers between devices, per_device(): lax.all_to_all(requests, 'drops', split_axis=0, concat_axis=0, tiled=True)  7.39 us
    ppermute x3, waiting for transfers between devices, per_device(): lax.ppermute(rows[r], 'wall', [(w, (w - r) % walls) for w in range(walls)])  4.76 us
    ppermute x3, starting transfers between devices, per_device(): lax.ppermute(wanted, 'wall', [(w, (w + r) % walls) for w in range(walls)])  4.21 us
    ppermute x3, starting transfers between devices, per_device(): lax.ppermute(rows[r], 'wall', [(w, (w - r) % walls) for w in range(walls)])  2.97 us
  transfers between devices with their start and end apart: 8, of which 3 were waited for; matrix products, arithmetic and copies ran while one was open for 10% of the time, Pallas kernels for 0%

commit v1 on v0

--- a/solution.py
+++ b/solution.py
@@ -84,10 +84,10 @@
     acc_ref[48:] += nn(two, lo)
 
 
-def finish(acc_ref, t_ref, b_ref, o_ref, drop):
+def finish(acc_ref, t_ref, b_ref, o_ref, drop, rest=None):
     q = acc_ref[0:16] + acc_ref[16:32] + acc_ref[32:48] + (acc_ref[48:64] + acc_ref[64:80])
     at = pl.ds(drop, 1)
-    x = [t_ref[i, at] for i in range(3)]
+    x = [t_ref[i, at][:, : acc_ref.shape[1]] for i in range(3)]
     square = x[0] * x[0] + x[1] * x[1] + x[2] * x[2]
     gs = [q[a : a + 1] for a in range(3)]
     h = [[q[3 + 3 * b + a : 4 + 3 * b + a] for a in range(3)] for b in range(3)]
@@ -97,6 +97,8 @@
         u = m[a] + square * gs[a] + x[a] * lean
         for b in range(3):
             u = u - x[b] * (2.0 * h[b][a] + h[a][b])
+        if rest is not None:
+            u = jnp.concatenate([u, rest[a]], axis=1)
         o_ref[a, at] = b_ref[a, at] + u
 
 
@@ -108,9 +110,160 @@
     finish(acc_ref, t_ref, b_ref, o_ref, drop)
 
 
+TILE = 256
+
+
+def upsample_rows(high, low, up_ref, f_ref):
+    depth, fine = up_ref.shape
+    rows = high.shape[0]
+    ks = range(0, depth, TILE)
+
+    def padded(v, shape):
+        for axis in range(2):
+            if v.shape[axis] < shape[axis]:
+                gap = list(v.shape)
+                gap[axis] = shape[axis] - v.shape[axis]
+                v = jnp.concatenate([v, jnp.zeros(gap, v.dtype)], axis=axis)
+        return v
+
+    parts = [
+        [padded(v[:, k : min(k + TILE, depth)], (rows, TILE)) for k in ks] for v in (high, low)
+    ]
+
+    def body(*accs):
+        pushed = [0, 0]
+
+        def push(m, value):
+            register = pushed[m] % 2
+            pushed[m] += 1
+            pltpu.matmul_push_rhs(value, staging_register=register, mxu_index=m)
+            return register
+
+        tiles = list(enumerate(range(0, fine, TILE)))
+
+        def flush(i, n0):
+            n1 = min(n0 + TILE, fine)
+            f = pltpu.matmul_pop(accs[i % 4])[:, : n1 - n0]
+            f_ref[:, :, n0:n1] = f.reshape(f_ref.shape[0], 8, n1 - n0)
+
+        for i, n0 in tiles:
+            m = i % 2
+            n1 = min(n0 + TILE, fine)
+            for j, k in enumerate(ks):
+                up = split(up_ref[k : min(k + TILE, depth), n0:n1], 2)
+                up = [padded(p, (TILE, TILE)) for p in up]
+                register = push(m, up[0])
+                pltpu.matmul_acc_lhs(accs[i % 4], parts[0][j], load_staged_rhs=register)
+                pltpu.matmul_acc_lhs(accs[i % 4], parts[1][j])
+                register = push(m, up[1])
+                pltpu.matmul_acc_lhs(accs[i % 4], parts[0][j], load_staged_rhs=register)
+            if i >= 2:
+                flush(*tiles[i - 2])
+        for tile in tiles[-2:]:
+            flush(*tile)
+
+    pl.run_scoped(body, *[pltpu.ACC(m)((rows, TILE), f32) for m in (0, 1, 0, 1)])
+
+
+def near_slot(row, width, xp_ref, acc_ref, u_ref, xb_ref, w_ref):
+    whole_chunks, half = divmod(width, TILE)
+    units = range(2)
+    cols = {}
+
+    def body(*refs):
+        main = [refs[0:3], refs[3:6]]
+        tail, high, low = refs[6:8], refs[8:10], refs[10:12]
+        pushed = [0, 0]
+
+        def push(m, value):
+            register = pushed[m] % 2
+            pushed[m] += 1
+            pltpu.matmul_push_rhs(value, staging_register=register, mxu_index=m)
+            return register
+
+        def start(chunks):
+            lhs = []
+            for c in chunks:
+                size = TILE if c < whole_chunks else half
+                dist, three, two = source_rows(lambda r: row(r, c * TILE, size))
+                cols[c] = three, two
+                turned = jnp.concatenate([dist, jnp.zeros((96, size), bf16)], axis=0).T
+                lhs.append(jnp.concatenate([turned, jnp.zeros((size, 128), bf16)], axis=1))
+            for m in units:
+                register = push(m, xp_ref[m])
+                for c, value in zip(chunks, lhs):
+                    into = main[m][c % 3] if c < whole_chunks else tail[m]
+                    pltpu.matmul_acc_lhs(into, value, load_staged_rhs=register)
+                    register = None
+
+        def cube(c, m):
+            w = lax.rsqrt(pltpu.matmul_pop(main[m][c % 3] if c < whole_chunks else tail[m]))
+            return split(w * w * w, 2)
+
+        def keep(c, m):
+            hi, lo = cube(c, m)
+            w_ref[c % 2, m, 0] = hi
+            w_ref[c % 2, m, 1] = lo
+
+        def reduce(c, m):
+            three, two = cols[c]
+            register = push(m, w_ref[c % 2, m, 0])
+            pltpu.matmul_acc_lhs(high[m], three, load_staged_rhs=register)
+            register = push(m, w_ref[c % 2, m, 1])
+            pltpu.matmul_acc_lhs(low[m], two, load_staged_rhs=register)
+
+        last = whole_chunks + (1 if half else 0)
+        start([0])
+        for c in range(whole_chunks):
+            if c % 2 == 0 and c + 1 < last:
+                start([k for k in (c + 1, c + 2) if k < last])
+            keep(c, 0)
+            if c > 0:
+                reduce(c - 1, 1)
+            keep(c, 1)
+            reduce(c, 0)
+        reduce(whole_chunks - 1, 1)
+        if half:
+            three, two = cols[whole_chunks]
+            two = jnp.concatenate([two, jnp.zeros((16, half), bf16)], axis=0)
+            both = jnp.concatenate([three, two], axis=1)
+            for m in units:
+                hi, lo = cube(whole_chunks, m)
+                register = push(m, jnp.concatenate([hi, lo], axis=0))
+                pltpu.matmul_acc_lhs(high[m], both, load_staged_rhs=register)
+        for m in units:
+            at = slice(m * TILE, (m + 1) * TILE)
+            acc_ref[:48, at] += pltpu.matmul_pop(high[m])
+            acc_ref[48:, at] += pltpu.matmul_pop(low[m])
+
+    acc = pltpu.ACC
+    pl.run_scoped(
+        body,
+        *[acc(m)((TILE, TILE), f32) for m in (0, 0, 0, 1, 1, 1)],
+        *[acc(m)((128, TILE), f32) for m in units],
+        *[acc(m)((48, TILE), f32) for m in units],
+        *[acc(m)((32, TILE), f32) for m in units],
+    )
+
+    x = [xb_ref[i] for i in range(3)]
+    u = [u_ref[i] for i in range(3)]
+    for s0 in range(0, width, 128):
+        y = [row(i, s0, 128) for i in range(3)]
+        g = [row(3 + i, s0, 128) for i in range(3)]
+        d = [x[i] - y[i] for i in range(3)]
+        r = d[0] * d[0] + d[1] * d[1] + d[2] * d[2] + smoothing_square
+        w = lax.rsqrt(r)
+        w3 = w * w * w
+        along = (d[0] * g[0] + d[1] * g[1] + d[2] * g[2]) * w3
+        plain = (r + smoothing_square) * w3
+        u = [u[i] + (plain * g[i] + along * d[i]) for i in range(3)]
+    for i in range(3):
+        u_ref[i] = u[i]
+
+
 def near_kernel(
     count_ref, pick_ref, got_ref, up_ref, t_ref, b_ref, o_ref,
-    cbuf, f_ref, acc_ref, xf_ref,
+    cbuf, f_ref, acc_ref, xp_ref, u_ref, xb_ref, w_ref,
 ):
     drop = pl.program_id(0)
     slot = pl.program_id(1)
@@ -119,6 +272,8 @@
     depth = got_ref.shape[2]
     coarse = got_ref.shape[3]
     fine = up_ref.shape[1]
+    tiled = 2 * TILE
+    rest = coarse - tiled
 
     @pl.when((drop == 0) & (slot == 0))
     def _():
@@ -132,12 +287,7 @@
             cbuf[e] = jnp.concatenate([row, pad], axis=0)
         source = cbuf[...]
         high, low = split(source.reshape(entries * 8, coarse), 2)
-        step = 384
-        for u0 in range(0, fine, step):
-            u1 = min(fine, u0 + step)
-            up = split(up_ref[:, u0:u1], 2)
-            f = nn(high, up[0]) + (nn(low, up[0]) + nn(high, up[1]))
-            f_ref[:, :, u0:u1] = f.reshape(entries, 8, u1 - u0)
+        upsample_rows(high, low, up_ref, f_ref)
         tail = f_ref.shape[2] - fine - coarse
         at = lax.broadcasted_iota(jnp.int32, source.shape, 1)
         source = jnp.where(at < 3, source, -source)
@@ -145,18 +295,35 @@
             [source, jnp.zeros((entries, 8, tail), f32)], axis=2
         )
 
+        xp_ref[...] = jnp.zeros_like(xp_ref)
+
     @pl.when(slot == 0)
     def _():
-        xf_ref[...] = target_rows([t_ref[i, pl.ds(drop, 1)] for i in range(3)])
+        x = [t_ref[i, pl.ds(drop, 1)] for i in range(3)]
+        feats = target_rows([v[:, :tiled] for v in x])
+        for m in range(2):
+            xp_ref[m, :32] = feats[:, m * TILE : (m + 1) * TILE]
+        for i in range(3):
+            end = jnp.concatenate([x[i][:, tiled:], jnp.zeros((1, 128 - rest), f32)], axis=1)
+            xb_ref[i] = jnp.broadcast_to(end, (128, 128)).T[:rest]
         acc_ref[...] = jnp.zeros_like(acc_ref)
+        u_ref[...] = jnp.zeros_like(u_ref)
 
     @pl.when(slot < count_ref[drop])
     def _():
-        accumulate(acc_ref, xf_ref[...], lambda c: f_ref[drop * slots + slot, c : c + 1])
+        entry = drop * slots + slot
+        near_slot(
+            lambda c, s0, size: f_ref[entry, c : c + 1, s0 : s0 + size],
+            f_ref.shape[2], xp_ref, acc_ref, u_ref, xb_ref, w_ref,
+        )
 
     @pl.when(slot == slots - 1)
     def _():
-        finish(acc_ref, t_ref, b_ref, o_ref, drop)
+        blank = jnp.zeros((128 - 3 * rest, 128), f32)
+        sums = jnp.concatenate([u_ref[0], u_ref[1], u_ref[2], blank], axis=0).T
+        line = jnp.sum(sums, axis=0, keepdims=True)
+        ends = [line[:, i * rest : (i + 1) * rest] for i in range(3)]
+        finish(acc_ref, t_ref, b_ref, o_ref, drop, ends)
 
 
 def whole(a):
@@ -194,8 +361,11 @@
             scratch_shapes=[
                 pltpu.VMEM((entries, 8, nodes), f32),
                 pltpu.VMEM((entries, 8, width), f32),
-                pltpu.VMEM((80, nodes), f32),
-                pltpu.VMEM((32, nodes), bf16),
+                pltpu.VMEM((80, 2 * TILE), f32),
+                pltpu.VMEM((2, TILE, TILE), bf16),
+                pltpu.VMEM((3, nodes - 2 * TILE, 128), f32),
+                pltpu.VMEM((3, nodes - 2 * TILE, 128), f32),
+                pltpu.VMEM((2, 2, 2, TILE, TILE), bf16),
             ],
         ),
         out_shape=jax.ShapeDtypeStruct(targets.shape, f32),
@@ -259,9 +429,8 @@
     mine = mine.reshape(owned, listed, 6, patch).transpose(0, 2, 1, 3).reshape(owned, 6, -1)
 
     targets = drop_points.transpose(1, 0, 2)
-    total = near_sums(
-        near_count, owner * depth + position, got, upsample, targets, base_velocity.transpose(1, 0, 2)
-    )
+    pick = owner * depth + position
+    total = near_sums(near_count, pick, got, upsample, targets, base_velocity.transpose(1, 0, 2))
     total = wall_sums(mine, targets, total)
     return total.transpose(1, 0, 2)
 

time: 143 us -> 137 us (0.958)
  Pallas kernels: 91.7 us -> 84.9 us
    pallas_call x1, Pallas kernels: 84.1 us -> 77.3 us  [near_sums(): pl.pallas_call(near_kernel, grid_spec=pltpu.PrefetchScalarGridSpec(num_sc...]
where the time goes in v1:
time: 137 us; the launch traced here: 136 us
  Pallas kernels  84.9 us (62%)
  starting transfers between devices  22.8 us (17%)
  local copies, waits for them, and re-layouts  17.2 us (13%)
  other arithmetic  6.05 us (4%)
  waiting for transfers between devices  4.77 us (3%)
    pallas_call x1, Pallas kernels, near_sums(): pl.pallas_call(near_kernel, grid_spec=pltpu.PrefetchScalarGridSpec(num_sc...  77.3 us
    all_to_all x1, starting transfers between devices, per_device(): got = lax.all_to_all(send, 'drops', split_axis=0, concat_axis=0, tiled=True)  8.23 us
    unnamed x7, local copies, waits for them, and re-layouts  8.1 us
    pallas_call x1, Pallas kernels, wall_sums(): pl.pallas_call(wall_kernel, grid=(owned,), in_specs=[whole(wall), whole(t...  7.55 us
    all_to_all x1, starting transfers between devices, per_device(): lax.all_to_all(requests, 'drops', split_axis=0, concat_axis=0, tiled=True)  7.39 us
    ppermute x3, waiting for transfers between devices, per_device(): lax.ppermute(rows[r], 'wall', [(w, (w - r) % walls) for w in range(walls)])  4.76 us
    ppermute x3, starting transfers between devices, per_device(): lax.ppermute(wanted, 'wall', [(w, (w + r) % walls) for w in range(walls)])  4.21 us
    ppermute x3, starting transfers between devices, per_device(): lax.ppermute(rows[r], 'wall', [(w, (w - r) % walls) for w in range(walls)])  2.97 us
  transfers between devices with their start and end apart: 8, of which 3 were waited for; matrix products, arithmetic and copies ran while one was open for 10% of the time, Pallas kernels for 0%

profile of v1, /device:TPU:113, one launch (start us, length us, event | category | flops | bytes accessed | tf_op | source)
XLA Modules:
  0.0 136.0 jit_solution(7370206154567690363)
XLA Ops:
  0.0 0.8 copy.39
  2.0 7.4 %all-to-all-start = ((s32[32,1,2]{2,1,0:T(1,128)}), s32[32,1,2]{2,1,0:T(1,128)S(1)}, u32[]{:S(2)}, u32[]{:S(2)}) async-start(s32[32,1,2]{2,1,0:T(1,128)} %copy.40), calls=%async_computation | async-start | bytes 32768 | tf_op jit(solution)/shard_map/all_to_all | solution.py:404
  10.0 0.8 reshape.180
  10.7 0.9 copy.44
  11.6 0.9 copy.43
  12.4 2.8 %copy.47 = f32[2048,192]{1,0:T(8,128)} copy(f32[2048,192]{0,1:T(8,128)} %param.17) | data formatting | bytes 3145728 | tf_op args[6]
  15.3 1.8 %copy.48 = f32[2048,192]{1,0:T(8,128)S(1)} copy(f32[2048,192]{0,1:T(8,128)} %param.18) | data formatting | bytes 3145728 | tf_op args[7]
  18.7 1.7 %gather_fusion = f32[64,6,544]{2,1,0:T(8,128)} fusion(f32[8,6,544]{2,1,0:T(8,128)S(1)} %pad_maximum_fusion, s32[1024]{0:T(1024)S(1)} %pad_clamp_fusion.1), kind=kCustom, calls=%fused_computation.2 | custom fusion | bytes 1671424 | tf_op jit(solution)/shard_map/jit(_take)/gather | solution.py:407
  20.4 2.9 %fusion = f32[32,6,2,544]{3,2,1,0:T(2,128)} fusion(f32[32,2,6,544]{3,2,1,0:T(8,128)} %bitcast.14, pred[32,2]{1,0:T(8,128)(4,1)S(1)} %copy.42), kind=kLoop, calls=%fused_computation.4 | loop fusion | flops 208896 | bytes 1671232 | tf_op jit(solution)/shard_map/transpose | solution.py:408
  23.4 1.2 collective-permute-start
  24.6 1.5 %collective-permute-start.2 = (s32[64]{0:T(128)S(1)}, s32[64]{0:T(128)S(1)}, u32[]{:S(2)}, u32[]{:S(2)}) collective-permute-start(s32[64]{0:T(128)S(1)} %reshape.180), channel_id=1, source_target_pairs={{0,96},{32,0},{64,32},{96,64},{1,97},{33,1},{65,33},{97,65},{2,98}... | collective-permute-start | bytes 776 | tf_op jit(solution)/shard_map/ppermute | solution.py:416
  26.0 1.5 %collective-permute-start.1 = (s32[64]{0:T(128)S(1)}, s32[64]{0:T(128)S(1)}, u32[]{:S(2)}, u32[]{:S(2)}) collective-permute-start(s32[64]{0:T(128)S(1)} %reshape.180), channel_id=1, source_target_pairs={{0,64},{32,96},{64,0},{96,32},{1,65},{33,97},{65,1},{97,33},{2,66}... | collective-permute-start | bytes 776 | tf_op jit(solution)/shard_map/ppermute | solution.py:416
  27.6 8.2 %all-to-all-start.1 = ((f32[32,6,2,544]{3,2,1,0:T(2,128)}), f32[32,6,2,544]{3,2,1,0:T(2,128)S(1)}, u32[]{:S(2)}, u32[]{:S(2)}) async-start(f32[32,6,2,544]{3,2,1,0:T(2,128)} %fusion), calls=%async_computation.1 | async-start | bytes 1966080 | tf_op jit(solution)/shard_map/all_to_all | solution.py:413
  36.0 2.6 %gather_fusion.1 = f32[256,192]{1,0:T(8,128)S(1)} fusion(f32[2048,192]{1,0:T(8,128)} %copy.47, s32[1024]{0:T(1024)S(1)} %pad_clamp_fusion), kind=kCustom, calls=%fused_computation.clone | custom fusion | bytes 394240 | tf_op jit(solution)/shard_map/jit(_take)/gather | solution.py:420
  38.5 1.7 %gather_fusion.2 = f32[256,192]{1,0:T(8,128)} fusion(f32[2048,192]{1,0:T(8,128)S(1)} %copy.48, s32[1024]{0:T(1024)S(1)} %pad_clamp_fusion), kind=kCustom, calls=%fused_computation.1.clone | custom fusion | bytes 394240 | tf_op jit(solution)/shard_map/jit(_take)/gather | solution.py:420
  40.2 1.1 broadcast_select_fusion
  41.4 0.9 collective-permute-start.5
  42.9 1.4 %collective-permute-start.4 = (f32[64,384]{1,0:T(8,128)S(1)}, f32[64,384]{1,0:T(8,128)S(1)}, u32[]{:S(2)}, u32[]{:S(2)}) collective-permute-start(f32[64,384]{1,0:T(8,128)S(1)} %get-tuple-element.16), channel_id=1, source_target_pairs={{0,64},{32,96},{64,0},{96,32},{1,65},{33,97},{65,1},{97,33},{2,66}... | collective-permute-start | bytes 294920 | tf_op jit(solution)/shard_map/ppermute | solution.py:426
  44.3 1.1 collective-permute-done.5
  45.4 2.1 %collective-permute-done.3 = f32[64,384]{1,0:T(8,128)S(1)} collective-permute-done((f32[64,384]{1,0:T(8,128)S(1)}, f32[64,384]{1,0:T(8,128)S(1)}, u32[]{:S(2)}, u32[]{:S(2)}) %collective-permute-start.3) | collective-permute-done | bytes 98336 | tf_op jit(solution)/shard_map/ppermute | solution.py:426
  47.5 1.6 %collective-permute-done.4 = f32[64,384]{1,0:T(8,128)S(1)} collective-permute-done((f32[64,384]{1,0:T(8,128)S(1)}, f32[64,384]{1,0:T(8,128)S(1)}, u32[]{:S(2)}, u32[]{:S(2)}) %collective-permute-start.4) | collective-permute-done | bytes 98336 | tf_op jit(solution)/shard_map/ppermute | solution.py:426
  50.1 1.0 copy-done
  51.1 77.3 %near_pairs.1.b_ref = f32[3,8,544]{2,1,0:T(8,128)} custom-call(s32[8]{0:T(128)} %count_ref.1, s32[32]{0:T(128)} %multiply_add_fusion.pick_ref, f32[32,6,2,544]{3,2,1,0:T(2,128)} %copy-done, f32[544,2112]{1,0:T(8,128)} %up_ref.1, f32[3,8,544]{2,1,0:T(8,128)} %bitcast.16, f32[3,8,544]{2,1,0:T(8,128)} %bitcast.18), custom_call_target="tpu_custom_call" | custom-call | tf_op jit(solution)/shard_map/near_pairs/pallas_call | solution.py:354
  128.4 7.6 %wall_pairs.1 = f32[3,8,544]{2,1,0:T(8,128)} custom-call(f32[8,6,512]{2,1,0:T(8,128)} %reshape.216.wall_ref, f32[3,8,544]{2,1,0:T(8,128)} %bitcast.17, f32[3,8,544]{2,1,0:T(8,128)} %near_pairs.1.b_ref), custom_call_target="tpu_custom_call" | custom-call | tf_op jit(solution)/shard_map/wall_pairs/pallas_call | solution.py:336
  (34 shorter events, 5.2 us)
Async XLA Ops:
  2.0 15.2 %all-to-all-start = ((s32[32,1,2]{2,1,0:T(1,128)}), s32[32,1,2]{2,1,0:T(1,128)S(1)}, u32[]{:S(2)}, u32[]{:S(2)}) async-start(s32[32,1,2]{2,1,0:T(1,128)} %copy.40), calls=%async_computation | async-start | bytes 32768 | tf_op jit(solution)/shard_map/all_to_all | solution.py:404
  23.4 12.5 %collective-permute-start = (s32[64]{0:T(128)S(1)}, s32[64]{0:T(128)S(1)}, u32[]{:S(2)}, u32[]{:S(2)}) collective-permute-start(s32[64]{0:T(128)S(1)} %reshape.180), channel_id=1, source_target_pairs={{0,32},{32,64},{64,96},{96,0},{1,33},{33,65},{65,97},{97,1},{2,34}... | collective-permute-start | bytes 776 | tf_op jit(solution)/shard_map/ppermute | solution.py:416
  24.6 11.3 %collective-permute-start.2 = (s32[64]{0:T(128)S(1)}, s32[64]{0:T(128)S(1)}, u32[]{:S(2)}, u32[]{:S(2)}) collective-permute-start(s32[64]{0:T(128)S(1)} %reshape.180), channel_id=1, source_target_pairs={{0,96},{32,0},{64,32},{96,64},{1,97},{33,1},{65,33},{97,65},{2,98}... | collective-permute-start | bytes 776 | tf_op jit(solution)/shard_map/ppermute | solution.py:416
  26.0 9.8 %collective-permute-start.1 = (s32[64]{0:T(128)S(1)}, s32[64]{0:T(128)S(1)}, u32[]{:S(2)}, u32[]{:S(2)}) collective-permute-start(s32[64]{0:T(128)S(1)} %reshape.180), channel_id=1, source_target_pairs={{0,64},{32,96},{64,0},{96,32},{1,65},{33,97},{65,1},{97,33},{2,66}... | collective-permute-start | bytes 776 | tf_op jit(solution)/shard_map/ppermute | solution.py:416
  27.6 22.5 %all-to-all-start.1 = ((f32[32,6,2,544]{3,2,1,0:T(2,128)}), f32[32,6,2,544]{3,2,1,0:T(2,128)S(1)}, u32[]{:S(2)}, u32[]{:S(2)}) async-start(f32[32,6,2,544]{3,2,1,0:T(2,128)} %fusion), calls=%async_computation.1 | async-start | bytes 1966080 | tf_op jit(solution)/shard_map/all_to_all | solution.py:413
  41.4 4.0 %collective-permute-start.5 = (f32[64,384]{1,0:T(8,128)S(1)}, f32[64,384]{1,0:T(8,128)S(1)}, u32[]{:S(2)}, u32[]{:S(2)}) collective-permute-start(f32[64,384]{1,0:T(8,128)S(1)} %get-tuple-element.14), channel_id=1, source_target_pairs={{0,96},{32,0},{64,32},{96,64},{1,97},{33,1},{65,33},{97,65},{2,98}... | collective-permute-start | bytes 294920 | tf_op jit(solution)/shard_map/ppermute | solution.py:426
  42.3 5.2 %collective-permute-start.3 = (f32[64,384]{1,0:T(8,128)S(1)}, f32[64,384]{1,0:T(8,128)S(1)}, u32[]{:S(2)}, u32[]{:S(2)}) collective-permute-start(f32[64,384]{1,0:T(8,128)S(1)} %get-tuple-element.15), channel_id=1, source_target_pairs={{0,32},{32,64},{64,96},{96,0},{1,33},{33,65},{65,97},{97,1},{2,34}... | collective-permute-start | bytes 294920 | tf_op jit(solution)/shard_map/ppermute | solution.py:426
  42.9 6.2 %collective-permute-start.4 = (f32[64,384]{1,0:T(8,128)S(1)}, f32[64,384]{1,0:T(8,128)S(1)}, u32[]{:S(2)}, u32[]{:S(2)}) collective-permute-start(f32[64,384]{1,0:T(8,128)S(1)} %get-tuple-element.16), channel_id=1, source_target_pairs={{0,64},{32,96},{64,0},{96,32},{1,65},{33,97},{65,1},{97,33},{2,66}... | collective-permute-start | bytes 294920 | tf_op jit(solution)/shard_map/ppermute | solution.py:426
  50.1 1.0 copy-start

commit v2 on v1

--- a/solution.py
+++ b/solution.py
@@ -373,6 +373,94 @@
     )(counts, pick, got, upsample, targets, base)
 
 
+def request_kernel(near_ref, ask_ref, pick_ref, seen_ref):
+    ranks, _, depth = ask_ref.shape
+    owned, slots = near_ref.shape
+    for r in range(ranks):
+        seen_ref[r] = 0
+        for p in range(depth):
+            ask_ref[r, 0, p] = 0
+    for e in range(owned * slots):
+        partner = near_ref[e // slots, e % slots]
+        owner = partner // owned % ranks
+        place = seen_ref[owner]
+        seen_ref[owner] = place + 1
+        ask_ref[owner, 0, place] = partner % owned
+        pick_ref[e] = owner * depth + place
+
+
+def make_requests(near_drops, ranks, depth):
+    owned, slots = near_drops.shape
+    smem = pl.BlockSpec(memory_space=pltpu.SMEM)
+    return pl.pallas_call(
+        request_kernel,
+        in_specs=[smem],
+        out_specs=[smem, smem],
+        out_shape=[
+            jax.ShapeDtypeStruct((ranks, 1, depth), jnp.int32),
+            jax.ShapeDtypeStruct((owned * slots,), jnp.int32),
+        ],
+        scratch_shapes=[pltpu.SMEM((ranks,), jnp.int32)],
+        name="requests",
+    )(near_drops)
+
+
+def send_kernel(ask_ref, pts_ref, str_ref, o_ref):
+    ranks, _, depth, _ = o_ref.shape
+    for r in range(ranks):
+        for p in range(depth):
+            at = pl.ds(ask_ref[r, 0, p], 1)
+            o_ref[r, 0:3, p : p + 1] = pts_ref[:, at]
+            o_ref[r, 3:6, p : p + 1] = str_ref[:, at]
+
+
+def gather_drops(incoming, points, strength):
+    ranks, _, depth = incoming.shape
+    shape = (ranks, 6, depth, points.shape[2])
+    return pl.pallas_call(
+        send_kernel,
+        grid_spec=pltpu.PrefetchScalarGridSpec(
+            num_scalar_prefetch=1,
+            grid=(1,),
+            in_specs=[whole(points), whole(strength)],
+            out_specs=pl.BlockSpec(shape, lambda *_: (0,) * 4, pipeline_mode=pl.Buffered(1)),
+        ),
+        out_shape=jax.ShapeDtypeStruct(shape, f32),
+        name="send_rows",
+    )(incoming, points, strength)
+
+
+def patch_kernel(index_ref, pts_ref, str_ref, *outs):
+    held = pts_ref.shape[1]
+    count = index_ref.shape[1]
+    step = 512
+    index = jnp.broadcast_to(index_ref[...], (step, count))
+    total = None
+    for k in range(0, held, step):
+        place = lax.broadcasted_iota(jnp.int32, (step, count), 0) + k
+        hot = jnp.where(place == index, 1.0, 0.0).astype(bf16)
+        rows = jnp.concatenate([pts_ref[:, k : k + step], str_ref[:, k : k + step]], axis=0)
+        part = [nn(p, hot) for p in split(rows, 3)]
+        part = part[0] + part[1] + part[2]
+        total = part if total is None else total + part
+    total = total.T
+    each = outs[0].shape[0]
+    for r, out in enumerate(outs):
+        out[...] = total[r * each : (r + 1) * each]
+
+
+def gather_patches(index, points, strength, walls):
+    n = index.shape[1] // walls
+    shape = jax.ShapeDtypeStruct((n, 2 * points.shape[0]), f32)
+    return pl.pallas_call(
+        patch_kernel,
+        in_specs=[whole(index), whole(points), whole(strength)],
+        out_specs=[whole(shape)] * walls,
+        out_shape=[shape] * walls,
+        name="patch_rows",
+    )(index, points, strength)
+
+
 def per_device(
     drop_points,
     drop_strength,
@@ -386,50 +474,35 @@
 ):
     ranks = lax.axis_size("drops")
     walls = lax.axis_size("wall")
-    owned, _, coarse = drop_points.shape
+    owned, _, _ = drop_points.shape
     slots = near_drops.shape[1]
     entries = owned * slots
     depth = max(2, (entries + ranks - 1) // ranks)
     here = lax.axis_index("wall")
 
-    partner = near_drops.reshape(entries)
-    owner = partner // owned % ranks
-    local = partner % owned
-    member = (owner[:, None] == jnp.arange(ranks, dtype=jnp.int32)[None, :]).astype(jnp.int32)
-    position = jnp.sum((jnp.cumsum(member, axis=0) - 1) * member, axis=1)
-    slot_hit = member[:, :, None] * (
-        position[:, None, None] == jnp.arange(depth, dtype=jnp.int32)[None, None, :]
-    ).astype(jnp.int32)
-    requests = jnp.sum(slot_hit * local[:, None, None], axis=0)
+    targets = drop_points.transpose(1, 0, 2)
+
+    requests, pick = make_requests(near_drops, ranks, depth)
     incoming = lax.all_to_all(requests, "drops", split_axis=0, concat_axis=0, tiled=True)
-
-    both = jnp.concatenate([drop_points, drop_strength], axis=1)
-    send = jnp.take(both, incoming.reshape(ranks * depth), axis=0)
-    send = send.reshape(ranks, depth, 6, coarse).transpose(0, 2, 1, 3)
+    send = gather_drops(incoming, targets, drop_strength.transpose(1, 0, 2))
 
     held = patch_points.shape[0]
     listed = wall_near.shape[1]
-    wanted, send = lax.optimization_barrier((wall_near.reshape(owned * listed), send))
+    wanted = wall_near.reshape(owned * listed)
     got = lax.all_to_all(send, "drops", split_axis=0, concat_axis=0, tiled=True)
     asked = [wanted]
     for r in range(1, walls):
         asked.append(lax.ppermute(wanted, "wall", [(w, (w + r) % walls) for w in range(walls)]))
 
-    index = jnp.clip(jnp.concatenate(asked) - here * held, 0, held - 1)
-    rows = jnp.concatenate(
-        [jnp.take(patch_points, index, axis=0), jnp.take(patch_strength, index, axis=0)], axis=1
-    )
-    rows = rows.reshape(walls, owned * listed, -1)
-    home = wanted // held
+    index = (jnp.concatenate(asked) - here * held)[None]
+    rows = gather_patches(index, patch_points.T, patch_strength.T, walls)
     mine = rows[0]
     for r in range(1, walls):
         back = lax.ppermute(rows[r], "wall", [(w, (w - r) % walls) for w in range(walls)])
-        mine = jnp.where((home == (here + r) % walls)[:, None], back, mine)
-    patch = rows.shape[2] // 6
+        mine = mine + back
+    patch = mine.shape[1] // 6
     mine = mine.reshape(owned, listed, 6, patch).transpose(0, 2, 1, 3).reshape(owned, 6, -1)
 
-    targets = drop_points.transpose(1, 0, 2)
-    pick = owner * depth + position
     total = near_sums(near_count, pick, got, upsample, targets, base_velocity.transpose(1, 0, 2))
     total = wall_sums(mine, targets, total)
     return total.transpose(1, 0, 2)

time: 137 us -> 132 us (0.964)
  the two profiles are of different devices: /device:TPU:113 before, /device:TPU:34 now
where the time goes in v2:
time: 132 us; the launch traced here: 131 us
  Pallas kernels  91.8 us (70%)
  blocking collectives  14.4 us (11%)
  starting transfers between devices  13.8 us (10%)
  waiting for transfers between devices  6.23 us (5%)
  local copies, waits for them, and re-layouts  3.35 us (3%)
  other arithmetic  1.56 us (1%)
    pallas_call x1, Pallas kernels, near_sums(): pl.pallas_call(near_kernel, grid_spec=pltpu.PrefetchScalarGridSpec(num_sc...  75.1 us
    all_to_all x1, blocking collectives, per_device(): lax.all_to_all(requests, 'drops', split_axis=0, concat_axis=0, tiled=True)  14.4 us
    pallas_call x1, Pallas kernels, wall_sums(): pl.pallas_call(wall_kernel, grid=(owned,), in_specs=[whole(wall), whole(t...  7.55 us
    all_to_all x1, starting transfers between devices, per_device(): got = lax.all_to_all(send, 'drops', split_axis=0, concat_axis=0, tiled=True)  4.89 us
    ppermute x3, starting transfers between devices, per_device(): lax.ppermute(wanted, 'wall', [(w, (w + r) % walls) for w in range(walls)])  4.77 us
    ppermute x3, waiting for transfers between devices, per_device(): lax.ppermute(rows[r], 'wall', [(w, (w - r) % walls) for w in range(walls)])  4.54 us
    pallas_call x1, Pallas kernels, gather_patches(): pl.pallas_call(patch_kernel, in_specs=[whole(index), whole(points), whole...  4.21 us
    ppermute x3, starting transfers between devices, per_device(): lax.ppermute(rows[r], 'wall', [(w, (w - r) % walls) for w in range(walls)])  4.14 us
  transfers between devices with their start and end apart: 7, of which 4 were waited for; matrix products, arithmetic and copies ran while one was open for 2% of the time, Pallas kernels for 3%

profile of v2, /device:TPU:34, one launch (start us, length us, event | category | flops | bytes accessed | tf_op | source)
XLA Modules:
  0.0 131.2 jit_solution(11462516565194907793)
XLA Ops:
  0.0 1.4 %copy.13.near_ref = s32[8,4]{1,0:T(8,128)} copy(s32[8,4]{0,1:T(4,128)} %param.13) | data formatting | bytes 256 | tf_op args[4]
  1.4 1.9 %requests.1 = (s32[32,1,2]{2,1,0:T(1,128)}, s32[32]{0:T(128)}) custom-call(s32[8,4]{1,0:T(8,128)} %copy.13.near_ref), custom_call_target="tpu_custom_call" | custom-call | tf_op jit(solution)/shard_map/requests/pallas_call | solution.py:395
  3.3 14.4 %all_to_all.10.ask_ref = s32[32,1,2]{2,1,0:T(1,128)} all-to-all(s32[32,1,2]{2,1,0:T(1,128)} %get-tuple-element.16), channel_id=1, replica_groups=mesh['wall'=4,'drops'=32] {'drops'}, dimensions={0} | all-to-all | bytes 512 | tf_op jit(solution)/shard_map/all_to_all | solution.py:486
  17.7 3.1 %send_rows.1 = f32[32,6,2,544]{3,2,1,0:T(2,128)} custom-call(s32[32,1,2]{2,1,0:T(1,128)} %all_to_all.10.ask_ref, f32[3,8,544]{2,1,0:T(8,128)} %bitcast.15, f32[3,8,544]{2,1,0:T(8,128)} %bitcast.18), custom_call_target="tpu_custom_call" | custom-call | tf_op jit(solution)/shard_map/send_rows/pallas_call | solution.py:420
  20.8 4.9 %all-to-all-start.1 = ((f32[32,6,2,544]{3,2,1,0:T(2,128)}), f32[32,6,2,544]{3,2,1,0:T(2,128)S(1)}, u32[]{:S(2)}, u32[]{:S(2)}) async-start(f32[32,6,2,544]{3,2,1,0:T(2,128)} %send_rows.1), calls=%async_computation.1 | async-start | bytes 1966080 | tf_op jit(solution)/shard_map/all_to_all | solution.py:492
  25.7 0.1 reshape.65
  25.8 0.5 collective-permute-start.2
  26.3 2.4 %collective-permute-start.1 = (s32[64]{0:T(128)S(1)}, s32[64]{0:T(128)S(1)}, u32[]{:S(2)}, u32[]{:S(2)}) collective-permute-start(s32[64]{0:T(128)S(1)} %reshape.65), channel_id=1, source_target_pairs={{0,64},{32,96},{64,0},{96,32},{1,65},{33,97},{65,1},{97,33},{2,66}... | collective-permute-start | bytes 776 | tf_op jit(solution)/shard_map/ppermute | solution.py:495
  28.7 1.8 %collective-permute-start = (s32[64]{0:T(128)S(1)}, s32[64]{0:T(128)S(1)}, u32[]{:S(2)}, u32[]{:S(2)}) collective-permute-start(s32[64]{0:T(128)S(1)} %reshape.65), channel_id=1, source_target_pairs={{0,32},{32,64},{64,96},{96,0},{1,33},{33,65},{65,97},{97,1},{2,34}... | collective-permute-start | bytes 776 | tf_op jit(solution)/shard_map/ppermute | solution.py:495
  30.6 0.8 collective-permute-done.1
  31.4 0.9 collective-permute-done
  32.3 0.6 add_subtract_fusion.index_ref
  32.9 4.2 %patch_rows.1 = (f32[64,384]{1,0:T(8,128)}, f32[64,384]{1,0:T(8,128)}, f32[64,384]{1,0:T(8,128)}, f32[64,384]{1,0:T(8,128)}) custom-call(s32[1,256]{1,0:T(1,128)} %add_subtract_fusion.index_ref, f32[192,2048]{1,0:T(8,128)} %bitcast.12, f32[192,2048]{1,0:T(8,128)} %bitcast.13), custom_call_target="tpu_custom_call" | custom-call | tf_op jit(solution)/shard_map/patch_rows/pallas_call | solution.py:455
  37.2 2.4 %collective-permute-start.3 = (f32[64,384]{1,0:T(8,128)}, f32[64,384]{1,0:T(8,128)S(1)}, u32[]{:S(2)}, u32[]{:S(2)}) collective-permute-start(f32[64,384]{1,0:T(8,128)} %get-tuple-element.12), channel_id=1, source_target_pairs={{0,96},{32,0},{64,32},{96,64},{1,97},{33,1},{65,33},{97,65},{2,98}... | collective-permute-start | bytes 294920 | tf_op jit(solution)/shard_map/ppermute | solution.py:501
  39.5 0.9 collective-permute-start.4
  40.4 0.9 collective-permute-start.5
  41.3 0.7 collective-permute-done.3
  42.0 3.8 %collective-permute-done.4 = f32[64,384]{1,0:T(8,128)S(1)} collective-permute-done((f32[64,384]{1,0:T(8,128)}, f32[64,384]{1,0:T(8,128)S(1)}, u32[]{:S(2)}, u32[]{:S(2)}) %collective-permute-start.4) | collective-permute-done | bytes 98336 | tf_op jit(solution)/shard_map/ppermute | solution.py:501
  45.8 0.9 add_add_fusion
  46.8 0.1 reshape.66
  46.9 0.8 reshape.68.wall_ref
  47.7 0.9 copy-done
  48.6 75.1 %near_pairs.1.b_ref = f32[3,8,544]{2,1,0:T(8,128)} custom-call(s32[8]{0:T(128)} %count_ref.1, s32[32]{0:T(128)} %get-tuple-element.15.pick_ref, f32[32,6,2,544]{3,2,1,0:T(2,128)} %copy-done, f32[544,2112]{1,0:T(8,128)} %up_ref.1, f32[3,8,544]{2,1,0:T(8,128)} %bitcast.16, f32[3,8,544]{2,1,0:T(8,128)} %bitcast.19), custom_call_target="tpu_custom_call" | custom-call | tf_op jit(solution)/shard_map/near_pairs/pallas_call | solution.py:354
  123.7 7.6 %wall_pairs.1 = f32[3,8,544]{2,1,0:T(8,128)} custom-call(f32[8,6,512]{2,1,0:T(8,128)} %reshape.68.wall_ref, f32[3,8,544]{2,1,0:T(8,128)} %bitcast.17, f32[3,8,544]{2,1,0:T(8,128)} %near_pairs.1.b_ref), custom_call_target="tpu_custom_call" | custom-call | tf_op jit(solution)/shard_map/wall_pairs/pallas_call | solution.py:336
  (8 shorter events, 0.1 us)
Async XLA Ops:
  0.0 25.7 %copy-start.1 = (s32[8,8]{1,0:T(8,128)S(1)}, s32[8,8]{1,0:T(8,128)}, u32[]{:S(2)}) copy-start(s32[8,8]{1,0:T(8,128)} %param.17) | copy-start | bytes 772
  20.8 26.9 %all-to-all-start.1 = ((f32[32,6,2,544]{3,2,1,0:T(2,128)}), f32[32,6,2,544]{3,2,1,0:T(2,128)S(1)}, u32[]{:S(2)}, u32[]{:S(2)}) async-start(f32[32,6,2,544]{3,2,1,0:T(2,128)} %send_rows.1), calls=%async_computation.1 | async-start | bytes 1966080 | tf_op jit(solution)/shard_map/all_to_all | solution.py:492
  25.8 4.8 %collective-permute-start.2 = (s32[64]{0:T(128)S(1)}, s32[64]{0:T(128)S(1)}, u32[]{:S(2)}, u32[]{:S(2)}) collective-permute-start(s32[64]{0:T(128)S(1)} %reshape.65), channel_id=1, source_target_pairs={{0,96},{32,0},{64,32},{96,64},{1,97},{33,1},{65,33},{97,65},{2,98}... | collective-permute-start | bytes 776 | tf_op jit(solution)/shard_map/ppermute | solution.py:495
  26.3 5.1 %collective-permute-start.1 = (s32[64]{0:T(128)S(1)}, s32[64]{0:T(128)S(1)}, u32[]{:S(2)}, u32[]{:S(2)}) collective-permute-start(s32[64]{0:T(128)S(1)} %reshape.65), channel_id=1, source_target_pairs={{0,64},{32,96},{64,0},{96,32},{1,65},{33,97},{65,1},{97,33},{2,66}... | collective-permute-start | bytes 776 | tf_op jit(solution)/shard_map/ppermute | solution.py:495
  28.7 3.6 %collective-permute-start = (s32[64]{0:T(128)S(1)}, s32[64]{0:T(128)S(1)}, u32[]{:S(2)}, u32[]{:S(2)}) collective-permute-start(s32[64]{0:T(128)S(1)} %reshape.65), channel_id=1, source_target_pairs={{0,32},{32,64},{64,96},{96,0},{1,33},{33,65},{65,97},{97,1},{2,34}... | collective-permute-start | bytes 776 | tf_op jit(solution)/shard_map/ppermute | solution.py:495
  37.2 4.9 %collective-permute-start.3 = (f32[64,384]{1,0:T(8,128)}, f32[64,384]{1,0:T(8,128)S(1)}, u32[]{:S(2)}, u32[]{:S(2)}) collective-permute-start(f32[64,384]{1,0:T(8,128)} %get-tuple-element.12), channel_id=1, source_target_pairs={{0,96},{32,0},{64,32},{96,64},{1,97},{33,1},{65,33},{97,65},{2,98}... | collective-permute-start | bytes 294920 | tf_op jit(solution)/shard_map/ppermute | solution.py:501
  39.5 6.3 %collective-permute-start.4 = (f32[64,384]{1,0:T(8,128)}, f32[64,384]{1,0:T(8,128)S(1)}, u32[]{:S(2)}, u32[]{:S(2)}) collective-permute-start(f32[64,384]{1,0:T(8,128)} %get-tuple-element.13), channel_id=1, source_target_pairs={{0,64},{32,96},{64,0},{96,32},{1,65},{33,97},{65,1},{97,33},{2,66}... | collective-permute-start | bytes 294920 | tf_op jit(solution)/shard_map/ppermute | solution.py:501
  40.4 5.4 %collective-permute-start.5 = (f32[64,384]{1,0:T(8,128)}, f32[64,384]{1,0:T(8,128)S(1)}, u32[]{:S(2)}, u32[]{:S(2)}) collective-permute-start(f32[64,384]{1,0:T(8,128)} %get-tuple-element.14), channel_id=1, source_target_pairs={{0,32},{32,64},{64,96},{96,0},{1,33},{33,65},{65,97},{97,1},{2,34}... | collective-permute-start | bytes 294920 | tf_op jit(solution)/shard_map/ppermute | solution.py:501
  47.7 0.9 copy-start

commit v3 on v2

--- a/solution.py
+++ b/solution.py
@@ -73,18 +73,11 @@
     return jnp.concatenate(rows, axis=0).astype(bf16)
 
 
-def accumulate(acc_ref, xf, row):
-    dist_rows, three, two = source_rows(row)
-    dist = lax.dot_general(dist_rows, xf, (((0,), (0,)), ((), ())), preferred_element_type=f32)
-    w = lax.rsqrt(dist)
-    w3 = w * w * w
-    hi = w3.astype(bf16)
-    lo = (w3 - hi.astype(f32)).astype(bf16)
-    acc_ref[:48] += nn(three, hi)
-    acc_ref[48:] += nn(two, lo)
-
-
-def finish(acc_ref, t_ref, b_ref, o_ref, drop, rest=None):
+def finish(acc_ref, u_ref, t_ref, b_ref, o_ref, drop):
+    rest = u_ref.shape[1]
+    blank = jnp.zeros((128 - 3 * rest, 128), f32)
+    sums = jnp.concatenate([u_ref[0], u_ref[1], u_ref[2], blank], axis=0).T
+    line = jnp.sum(sums, axis=0, keepdims=True)
     q = acc_ref[0:16] + acc_ref[16:32] + acc_ref[32:48] + (acc_ref[48:64] + acc_ref[64:80])
     at = pl.ds(drop, 1)
     x = [t_ref[i, at][:, : acc_ref.shape[1]] for i in range(3)]
@@ -97,17 +90,8 @@
         u = m[a] + square * gs[a] + x[a] * lean
         for b in range(3):
             u = u - x[b] * (2.0 * h[b][a] + h[a][b])
-        if rest is not None:
-            u = jnp.concatenate([u, rest[a]], axis=1)
+        u = jnp.concatenate([u, line[:, a * rest : (a + 1) * rest]], axis=1)
         o_ref[a, at] = b_ref[a, at] + u
-
-
-def wall_kernel(wall_ref, t_ref, b_ref, o_ref, acc_ref):
-    drop = pl.program_id(0)
-    acc_ref[...] = jnp.zeros_like(acc_ref)
-    xf = target_rows([t_ref[i, pl.ds(drop, 1)] for i in range(3)])
-    accumulate(acc_ref, xf, lambda c: wall_ref[drop, c : c + 1])
-    finish(acc_ref, t_ref, b_ref, o_ref, drop)
 
 
 TILE = 256
@@ -261,21 +245,47 @@
         u_ref[i] = u[i]
 
 
+def set_targets(drop, t_ref, xp_ref, acc_ref, u_ref, xb_ref):
+    tiled = 2 * TILE
+    x = [t_ref[i, pl.ds(drop, 1)] for i in range(3)]
+    feats = target_rows([v[:, :tiled] for v in x])
+    for m in range(2):
+        xp_ref[m, :32] = feats[:, m * TILE : (m + 1) * TILE]
+    rest = xb_ref.shape[1]
+    for i in range(3):
+        end = jnp.concatenate([x[i][:, tiled:], jnp.zeros((1, 128 - rest), f32)], axis=1)
+        xb_ref[i] = jnp.broadcast_to(end, (128, 128)).T[:rest]
+    acc_ref[...] = jnp.zeros_like(acc_ref)
+    u_ref[...] = jnp.zeros_like(u_ref)
+
+
+def wall_kernel(wall_ref, t_ref, b_ref, o_ref, acc_ref, xp_ref, u_ref, xb_ref, w_ref):
+    xp_ref[...] = jnp.zeros_like(xp_ref)
+
+    def one_drop(drop, carry):
+        set_targets(drop, t_ref, xp_ref, acc_ref, u_ref, xb_ref)
+        near_slot(
+            lambda c, s0, size: wall_ref[drop, c : c + 1, s0 : s0 + size],
+            wall_ref.shape[2], xp_ref, acc_ref, u_ref, xb_ref, w_ref,
+        )
+        finish(acc_ref, u_ref, t_ref, b_ref, o_ref, drop)
+        return carry
+
+    lax.fori_loop(0, t_ref.shape[1], one_drop, 0)
+
+
 def near_kernel(
     count_ref, pick_ref, got_ref, up_ref, t_ref, b_ref, o_ref,
     cbuf, f_ref, acc_ref, xp_ref, u_ref, xb_ref, w_ref,
 ):
-    drop = pl.program_id(0)
-    slot = pl.program_id(1)
-    slots = pl.num_programs(1)
     entries = f_ref.shape[0]
+    owned = t_ref.shape[1]
+    slots = entries // owned
     depth = got_ref.shape[2]
     coarse = got_ref.shape[3]
     fine = up_ref.shape[1]
-    tiled = 2 * TILE
-    rest = coarse - tiled
-
-    @pl.when((drop == 0) & (slot == 0))
+
+    @pl.when(count_ref[0] >= 0)
     def _():
         pad = jnp.zeros((2, coarse), f32)
         for e in range(entries):
@@ -295,35 +305,24 @@
             [source, jnp.zeros((entries, 8, tail), f32)], axis=2
         )
 
-        xp_ref[...] = jnp.zeros_like(xp_ref)
-
-    @pl.when(slot == 0)
-    def _():
-        x = [t_ref[i, pl.ds(drop, 1)] for i in range(3)]
-        feats = target_rows([v[:, :tiled] for v in x])
-        for m in range(2):
-            xp_ref[m, :32] = feats[:, m * TILE : (m + 1) * TILE]
-        for i in range(3):
-            end = jnp.concatenate([x[i][:, tiled:], jnp.zeros((1, 128 - rest), f32)], axis=1)
-            xb_ref[i] = jnp.broadcast_to(end, (128, 128)).T[:rest]
-        acc_ref[...] = jnp.zeros_like(acc_ref)
-        u_ref[...] = jnp.zeros_like(u_ref)
-
-    @pl.when(slot < count_ref[drop])
-    def _():
-        entry = drop * slots + slot
-        near_slot(
-            lambda c, s0, size: f_ref[entry, c : c + 1, s0 : s0 + size],
-            f_ref.shape[2], xp_ref, acc_ref, u_ref, xb_ref, w_ref,
-        )
-
-    @pl.when(slot == slots - 1)
-    def _():
-        blank = jnp.zeros((128 - 3 * rest, 128), f32)
-        sums = jnp.concatenate([u_ref[0], u_ref[1], u_ref[2], blank], axis=0).T
-        line = jnp.sum(sums, axis=0, keepdims=True)
-        ends = [line[:, i * rest : (i + 1) * rest] for i in range(3)]
-        finish(acc_ref, t_ref, b_ref, o_ref, drop, ends)
+    xp_ref[...] = jnp.zeros_like(xp_ref)
+
+    def one_drop(drop, carry):
+        set_targets(drop, t_ref, xp_ref, acc_ref, u_ref, xb_ref)
+
+        def one_slot(slot, inner):
+            entry = drop * slots + slot
+            near_slot(
+                lambda c, s0, size: f_ref[entry, c : c + 1, s0 : s0 + size],
+                f_ref.shape[2], xp_ref, acc_ref, u_ref, xb_ref, w_ref,
+            )
+            return inner
+
+        lax.fori_loop(0, count_ref[drop], one_slot, 0)
+        finish(acc_ref, u_ref, t_ref, b_ref, o_ref, drop)
+        return carry
+
+    lax.fori_loop(0, owned, one_drop, 0)
 
 
 def whole(a):
@@ -331,43 +330,41 @@
     return pl.BlockSpec(a.shape, lambda *_: zeros, pipeline_mode=pl.Buffered(1))
 
 
+def sum_scratch(nodes):
+    return [
+        pltpu.VMEM((80, 2 * TILE), f32),
+        pltpu.VMEM((2, TILE, TILE), bf16),
+        pltpu.VMEM((3, nodes - 2 * TILE, 128), f32),
+        pltpu.VMEM((3, nodes - 2 * TILE, 128), f32),
+        pltpu.VMEM((2, 2, 2, TILE, TILE), bf16),
+    ]
+
+
 def wall_sums(wall, targets, base):
-    _, owned, nodes = targets.shape
     return pl.pallas_call(
         wall_kernel,
-        grid=(owned,),
         in_specs=[whole(wall), whole(targets), whole(base)],
         out_specs=whole(targets),
-        scratch_shapes=[
-            pltpu.VMEM((80, nodes), f32),
-        ],
+        scratch_shapes=sum_scratch(targets.shape[2]),
         out_shape=jax.ShapeDtypeStruct(targets.shape, f32),
         name="wall_pairs",
     )(wall, targets, base)
 
 
 def near_sums(counts, pick, got, upsample, targets, base):
-    _, owned, nodes = targets.shape
+    nodes = targets.shape[2]
     entries = pick.shape[0]
-    slots = entries // owned
     width = -(-(upsample.shape[1] + nodes) // 128) * 128
+    smem = pl.BlockSpec(memory_space=pltpu.SMEM)
     return pl.pallas_call(
         near_kernel,
-        grid_spec=pltpu.PrefetchScalarGridSpec(
-            num_scalar_prefetch=2,
-            grid=(owned, slots),
-            in_specs=[whole(got), whole(upsample), whole(targets), whole(base)],
-            out_specs=whole(targets),
-            scratch_shapes=[
-                pltpu.VMEM((entries, 8, nodes), f32),
-                pltpu.VMEM((entries, 8, width), f32),
-                pltpu.VMEM((80, 2 * TILE), f32),
-                pltpu.VMEM((2, TILE, TILE), bf16),
-                pltpu.VMEM((3, nodes - 2 * TILE, 128), f32),
-                pltpu.VMEM((3, nodes - 2 * TILE, 128), f32),
-                pltpu.VMEM((2, 2, 2, TILE, TILE), bf16),
-            ],
-        ),
+        in_specs=[smem, smem, whole(got), whole(upsample), whole(targets), whole(base)],
+        out_specs=whole(targets),
+        scratch_shapes=[
+            pltpu.VMEM((entries, 8, nodes), f32),
+            pltpu.VMEM((entries, 8, width), f32),
+            *sum_scratch(nodes),
+        ],
         out_shape=jax.ShapeDtypeStruct(targets.shape, f32),
         name="near_pairs",
     )(counts, pick, got, upsample, targets, base)

time: 132 us -> 130 us (0.985)
  Pallas kernels: 91.8 us -> 89.9 us
    pallas_call x2, Pallas kernels: 82.6 us -> 80.7 us  [the longest x1 73 us: near_sums(): pl.pallas_call(near_kernel, in_specs=[smem, smem, whole(got), whole(upsam...]
where the time goes in v3:
time: 130 us; the launch traced here: 129 us
  Pallas kernels  89.9 us (69%)
  blocking collectives  14.4 us (11%)
  starting transfers between devices  13.8 us (11%)
  waiting for transfers between devices  6.23 us (5%)
  local copies, waits for them, and re-layouts  3.35 us (3%)
  other arithmetic  1.56 us (1%)
    pallas_call x1, Pallas kernels, near_sums(): pl.pallas_call(near_kernel, in_specs=[smem, smem, whole(got), whole(upsam...  73 us
    all_to_all x1, blocking collectives, per_device(): lax.all_to_all(requests, 'drops', split_axis=0, concat_axis=0, tiled=True)  14.4 us
    pallas_call x1, Pallas kernels, wall_sums(): pl.pallas_call(wall_kernel, in_specs=[whole(wall), whole(targets), whole(...  7.73 us
    all_to_all x1, starting transfers between devices, per_device(): got = lax.all_to_all(send, 'drops', split_axis=0, concat_axis=0, tiled=True)  4.89 us
    ppermute x3, starting transfers between devices, per_device(): lax.ppermute(wanted, 'wall', [(w, (w + r) % walls) for w in range(walls)])  4.77 us
    ppermute x3, waiting for transfers between devices, per_device(): lax.ppermute(rows[r], 'wall', [(w, (w - r) % walls) for w in range(walls)])  4.54 us
    pallas_call x1, Pallas kernels, gather_patches(): pl.pallas_call(patch_kernel, in_specs=[whole(index), whole(points), whole...  4.21 us
    ppermute x3, starting transfers between devices, per_device(): lax.ppermute(rows[r], 'wall', [(w, (w - r) % walls) for w in range(walls)])  4.14 us
  transfers between devices with their start and end apart: 7, of which 4 were waited for; matrix products, arithmetic and copies ran while one was open for 2% of the time, Pallas kernels for 3%

profile of v3, /device:TPU:34, one launch (start us, length us, event | category | flops | bytes accessed | tf_op | source)
XLA Modules:
  0.0 129.3 jit_solution(12349928339827285061)
XLA Ops:
  0.0 1.4 %copy.13.near_ref = s32[8,4]{1,0:T(8,128)} copy(s32[8,4]{0,1:T(4,128)} %param.13) | data formatting | bytes 256 | tf_op args[4]
  1.4 1.9 %requests.1 = (s32[32,1,2]{2,1,0:T(1,128)}, s32[32]{0:T(128)}) custom-call(s32[8,4]{1,0:T(8,128)} %copy.13.near_ref), custom_call_target="tpu_custom_call" | custom-call | tf_op jit(solution)/shard_map/requests/pallas_call | solution.py:392
  3.3 14.4 %all_to_all.10.ask_ref = s32[32,1,2]{2,1,0:T(1,128)} all-to-all(s32[32,1,2]{2,1,0:T(1,128)} %get-tuple-element.16), channel_id=1, replica_groups=mesh['wall'=4,'drops'=32] {'drops'}, dimensions={0} | all-to-all | bytes 512 | tf_op jit(solution)/shard_map/all_to_all | solution.py:483
  17.7 3.1 %send_rows.1 = f32[32,6,2,544]{3,2,1,0:T(2,128)} custom-call(s32[32,1,2]{2,1,0:T(1,128)} %all_to_all.10.ask_ref, f32[3,8,544]{2,1,0:T(8,128)} %bitcast.15, f32[3,8,544]{2,1,0:T(8,128)} %bitcast.18), custom_call_target="tpu_custom_call" | custom-call | tf_op jit(solution)/shard_map/send_rows/pallas_call | solution.py:417
  20.8 4.9 %all-to-all-start.1 = ((f32[32,6,2,544]{3,2,1,0:T(2,128)}), f32[32,6,2,544]{3,2,1,0:T(2,128)S(1)}, u32[]{:S(2)}, u32[]{:S(2)}) async-start(f32[32,6,2,544]{3,2,1,0:T(2,128)} %send_rows.1), calls=%async_computation.1 | async-start | bytes 1966080 | tf_op jit(solution)/shard_map/all_to_all | solution.py:489
  25.7 0.1 reshape.65
  25.8 0.5 collective-permute-start.2
  26.3 2.4 %collective-permute-start.1 = (s32[64]{0:T(128)S(1)}, s32[64]{0:T(128)S(1)}, u32[]{:S(2)}, u32[]{:S(2)}) collective-permute-start(s32[64]{0:T(128)S(1)} %reshape.65), channel_id=1, source_target_pairs={{0,64},{32,96},{64,0},{96,32},{1,65},{33,97},{65,1},{97,33},{2,66}... | collective-permute-start | bytes 776 | tf_op jit(solution)/shard_map/ppermute | solution.py:492
  28.7 1.8 %collective-permute-start = (s32[64]{0:T(128)S(1)}, s32[64]{0:T(128)S(1)}, u32[]{:S(2)}, u32[]{:S(2)}) collective-permute-start(s32[64]{0:T(128)S(1)} %reshape.65), channel_id=1, source_target_pairs={{0,32},{32,64},{64,96},{96,0},{1,33},{33,65},{65,97},{97,1},{2,34}... | collective-permute-start | bytes 776 | tf_op jit(solution)/shard_map/ppermute | solution.py:492
  30.6 0.8 collective-permute-done.1
  31.4 0.9 collective-permute-done
  32.3 0.6 add_subtract_fusion.index_ref
  32.9 4.2 %patch_rows.1 = (f32[64,384]{1,0:T(8,128)}, f32[64,384]{1,0:T(8,128)}, f32[64,384]{1,0:T(8,128)}, f32[64,384]{1,0:T(8,128)}) custom-call(s32[1,256]{1,0:T(1,128)} %add_subtract_fusion.index_ref, f32[192,2048]{1,0:T(8,128)} %bitcast.12, f32[192,2048]{1,0:T(8,128)} %bitcast.13), custom_call_target="tpu_custom_call" | custom-call | tf_op jit(solution)/shard_map/patch_rows/pallas_call | solution.py:452
  37.2 2.4 %collective-permute-start.3 = (f32[64,384]{1,0:T(8,128)}, f32[64,384]{1,0:T(8,128)S(1)}, u32[]{:S(2)}, u32[]{:S(2)}) collective-permute-start(f32[64,384]{1,0:T(8,128)} %get-tuple-element.12), channel_id=1, source_target_pairs={{0,96},{32,0},{64,32},{96,64},{1,97},{33,1},{65,33},{97,65},{2,98}... | collective-permute-start | bytes 294920 | tf_op jit(solution)/shard_map/ppermute | solution.py:498
  39.5 0.9 collective-permute-start.4
  40.4 0.9 collective-permute-start.5
  41.3 0.7 collective-permute-done.3
  42.0 3.8 %collective-permute-done.4 = f32[64,384]{1,0:T(8,128)S(1)} collective-permute-done((f32[64,384]{1,0:T(8,128)}, f32[64,384]{1,0:T(8,128)S(1)}, u32[]{:S(2)}, u32[]{:S(2)}) %collective-permute-start.4) | collective-permute-done | bytes 98336 | tf_op jit(solution)/shard_map/ppermute | solution.py:498
  45.8 0.9 add_add_fusion
  46.8 0.1 reshape.66
  46.9 0.8 reshape.68.wall_ref
  47.7 0.9 copy-done
  48.6 73.0 %near_pairs.1.b_ref = f32[3,8,544]{2,1,0:T(8,128)} custom-call(s32[8]{0:T(128)} %count_ref.1, s32[32]{0:T(128)} %get-tuple-element.15.pick_ref, f32[32,6,2,544]{3,2,1,0:T(2,128)} %copy-done, f32[544,2112]{1,0:T(8,128)} %up_ref.1, f32[3,8,544]{2,1,0:T(8,128)} %bitcast.16, f32[3,8,544]{2,1,0:T(8,128)} %bitcast.19), custom_call_target="tpu_custom_call" | custom-call | tf_op jit(solution)/shard_map/near_pairs/pallas_call | solution.py:359
  121.6 7.7 %wall_pairs.1 = f32[3,8,544]{2,1,0:T(8,128)} custom-call(f32[8,6,512]{2,1,0:T(8,128)} %reshape.68.wall_ref, f32[3,8,544]{2,1,0:T(8,128)} %bitcast.17, f32[3,8,544]{2,1,0:T(8,128)} %near_pairs.1.b_ref), custom_call_target="tpu_custom_call" | custom-call | tf_op jit(solution)/shard_map/wall_pairs/pallas_call | solution.py:344
  (8 shorter events, 0.1 us)
Async XLA Ops:
  0.0 25.7 %copy-start.1 = (s32[8,8]{1,0:T(8,128)S(1)}, s32[8,8]{1,0:T(8,128)}, u32[]{:S(2)}) copy-start(s32[8,8]{1,0:T(8,128)} %param.17) | copy-start | bytes 772
  20.8 26.9 %all-to-all-start.1 = ((f32[32,6,2,544]{3,2,1,0:T(2,128)}), f32[32,6,2,544]{3,2,1,0:T(2,128)S(1)}, u32[]{:S(2)}, u32[]{:S(2)}) async-start(f32[32,6,2,544]{3,2,1,0:T(2,128)} %send_rows.1), calls=%async_computation.1 | async-start | bytes 1966080 | tf_op jit(solution)/shard_map/all_to_all | solution.py:489
  25.8 4.8 %collective-permute-start.2 = (s32[64]{0:T(128)S(1)}, s32[64]{0:T(128)S(1)}, u32[]{:S(2)}, u32[]{:S(2)}) collective-permute-start(s32[64]{0:T(128)S(1)} %reshape.65), channel_id=1, source_target_pairs={{0,96},{32,0},{64,32},{96,64},{1,97},{33,1},{65,33},{97,65},{2,98}... | collective-permute-start | bytes 776 | tf_op jit(solution)/shard_map/ppermute | solution.py:492
  26.3 5.1 %collective-permute-start.1 = (s32[64]{0:T(128)S(1)}, s32[64]{0:T(128)S(1)}, u32[]{:S(2)}, u32[]{:S(2)}) collective-permute-start(s32[64]{0:T(128)S(1)} %reshape.65), channel_id=1, source_target_pairs={{0,64},{32,96},{64,0},{96,32},{1,65},{33,97},{65,1},{97,33},{2,66}... | collective-permute-start | bytes 776 | tf_op jit(solution)/shard_map/ppermute | solution.py:492
  28.7 3.6 %collective-permute-start = (s32[64]{0:T(128)S(1)}, s32[64]{0:T(128)S(1)}, u32[]{:S(2)}, u32[]{:S(2)}) collective-permute-start(s32[64]{0:T(128)S(1)} %reshape.65), channel_id=1, source_target_pairs={{0,32},{32,64},{64,96},{96,0},{1,33},{33,65},{65,97},{97,1},{2,34}... | collective-permute-start | bytes 776 | tf_op jit(solution)/shard_map/ppermute | solution.py:492
  37.2 4.9 %collective-permute-start.3 = (f32[64,384]{1,0:T(8,128)}, f32[64,384]{1,0:T(8,128)S(1)}, u32[]{:S(2)}, u32[]{:S(2)}) collective-permute-start(f32[64,384]{1,0:T(8,128)} %get-tuple-element.12), channel_id=1, source_target_pairs={{0,96},{32,0},{64,32},{96,64},{1,97},{33,1},{65,33},{97,65},{2,98}... | collective-permute-start | bytes 294920 | tf_op jit(solution)/shard_map/ppermute | solution.py:498
  39.5 6.3 %collective-permute-start.4 = (f32[64,384]{1,0:T(8,128)}, f32[64,384]{1,0:T(8,128)S(1)}, u32[]{:S(2)}, u32[]{:S(2)}) collective-permute-start(f32[64,384]{1,0:T(8,128)} %get-tuple-element.13), channel_id=1, source_target_pairs={{0,64},{32,96},{64,0},{96,32},{1,65},{33,97},{65,1},{97,33},{2,66}... | collective-permute-start | bytes 294920 | tf_op jit(solution)/shard_map/ppermute | solution.py:498
  40.4 5.4 %collective-permute-start.5 = (f32[64,384]{1,0:T(8,128)}, f32[64,384]{1,0:T(8,128)S(1)}, u32[]{:S(2)}, u32[]{:S(2)}) collective-permute-start(f32[64,384]{1,0:T(8,128)} %get-tuple-element.14), channel_id=1, source_target_pairs={{0,32},{32,64},{64,96},{96,0},{1,33},{33,65},{65,97},{97,1},{2,34}... | collective-permute-start | bytes 294920 | tf_op jit(solution)/shard_map/ppermute | solution.py:498
  47.7 0.9 copy-start

commit v4 on v3

--- a/solution.py
+++ b/solution.py
@@ -271,7 +271,8 @@
         finish(acc_ref, u_ref, t_ref, b_ref, o_ref, drop)
         return carry
 
-    lax.fori_loop(0, t_ref.shape[1], one_drop, 0)
+    for drop in range(t_ref.shape[1]):
+        one_drop(drop, 0)
 
 
 def near_kernel(
@@ -372,13 +373,13 @@
 
 def request_kernel(near_ref, ask_ref, pick_ref, seen_ref):
     ranks, _, depth = ask_ref.shape
-    owned, slots = near_ref.shape
+    slots, owned = near_ref.shape
     for r in range(ranks):
         seen_ref[r] = 0
         for p in range(depth):
             ask_ref[r, 0, p] = 0
     for e in range(owned * slots):
-        partner = near_ref[e // slots, e % slots]
+        partner = near_ref[e % slots, e // slots]
         owner = partner // owned % ranks
         place = seen_ref[owner]
         seen_ref[owner] = place + 1
@@ -387,7 +388,7 @@
 
 
 def make_requests(near_drops, ranks, depth):
-    owned, slots = near_drops.shape
+    slots, owned = near_drops.shape
     smem = pl.BlockSpec(memory_space=pltpu.SMEM)
     return pl.pallas_call(
         request_kernel,
@@ -479,7 +480,7 @@
 
     targets = drop_points.transpose(1, 0, 2)
 
-    requests, pick = make_requests(near_drops, ranks, depth)
+    requests, pick = make_requests(near_drops.T, ranks, depth)
     incoming = lax.all_to_all(requests, "drops", split_axis=0, concat_axis=0, tiled=True)
     send = gather_drops(incoming, targets, drop_strength.transpose(1, 0, 2))
 

time: 130 us -> 127 us (0.977)
  local copies, waits for them, and re-layouts: 3.35 us -> 2 us
    pallas_call x1, Pallas kernels: 7.73 us -> 6.36 us  [wall_sums(): pl.pallas_call(wall_kernel, in_specs=[whole(wall), whole(targets), whole(...]
    unnamed x5 -> x4, local copies, waits for them, and re-layouts: 2.3 us -> 0.95 us
where the time goes in v4:
time: 127 us
  Pallas kernels  88.8 us (70%)
  blocking collectives  14.4 us (11%)
  starting transfers between devices  13.8 us (11%)
  waiting for transfers between devices  6.23 us (5%)
  local copies, waits for them, and re-layouts  2 us (2%)
  other arithmetic  1.56 us (1%)
    pallas_call x1, Pallas kernels, near_sums(): pl.pallas_call(near_kernel, in_specs=[smem, smem, whole(got), whole(upsam...  73.2 us
    all_to_all x1, blocking collectives, per_device(): lax.all_to_all(requests, 'drops', split_axis=0, concat_axis=0, tiled=True)  14.4 us
    pallas_call x1, Pallas kernels, wall_sums(): pl.pallas_call(wall_kernel, in_specs=[whole(wall), whole(targets), whole(...  6.36 us
    all_to_all x1, starting transfers between devices, per_device(): got = lax.all_to_all(send, 'drops', split_axis=0, concat_axis=0, tiled=True)  4.89 us
    ppermute x3, starting transfers between devices, per_device(): lax.ppermute(wanted, 'wall', [(w, (w + r) % walls) for w in range(walls)])  4.77 us
    ppermute x3, waiting for transfers between devices, per_device(): lax.ppermute(rows[r], 'wall', [(w, (w - r) % walls) for w in range(walls)])  4.54 us
    pallas_call x1, Pallas kernels, gather_patches(): pl.pallas_call(patch_kernel, in_specs=[whole(index), whole(points), whole...  4.21 us
    ppermute x3, starting transfers between devices, per_device(): lax.ppermute(rows[r], 'wall', [(w, (w - r) % walls) for w in range(walls)])  4.14 us
  transfers between devices with their start and end apart: 7, of which 4 were waited for; matrix products, arithmetic and copies ran while one was open for 2% of the time, Pallas kernels for 3%

profile of v4, /device:TPU:34, one launch (start us, length us, event | category | flops | bytes accessed | tf_op | source)
XLA Modules:
  0.0 126.9 jit_solution(15773503064701592548)
XLA Ops:
  0.0 2.0 %requests.1 = (s32[32,1,2]{2,1,0:T(1,128)}, s32[32]{0:T(128)}) custom-call(s32[4,8]{1,0:T(4,128)} %bitcast.21), custom_call_target="tpu_custom_call" | custom-call | tf_op jit(solution)/shard_map/requests/pallas_call | solution.py:393
  2.0 14.4 %all_to_all.10.ask_ref = s32[32,1,2]{2,1,0:T(1,128)} all-to-all(s32[32,1,2]{2,1,0:T(1,128)} %get-tuple-element.16), channel_id=1, replica_groups=mesh['wall'=4,'drops'=32] {'drops'}, dimensions={0} | all-to-all | bytes 512 | tf_op jit(solution)/shard_map/all_to_all | solution.py:484
  16.5 3.1 %send_rows.1 = f32[32,6,2,544]{3,2,1,0:T(2,128)} custom-call(s32[32,1,2]{2,1,0:T(1,128)} %all_to_all.10.ask_ref, f32[3,8,544]{2,1,0:T(8,128)} %bitcast.16, f32[3,8,544]{2,1,0:T(8,128)} %bitcast.19), custom_call_target="tpu_custom_call" | custom-call | tf_op jit(solution)/shard_map/send_rows/pallas_call | solution.py:418
  19.5 4.9 %all-to-all-start.1 = ((f32[32,6,2,544]{3,2,1,0:T(2,128)}), f32[32,6,2,544]{3,2,1,0:T(2,128)S(1)}, u32[]{:S(2)}, u32[]{:S(2)}) async-start(f32[32,6,2,544]{3,2,1,0:T(2,128)} %send_rows.1), calls=%async_computation.1 | async-start | bytes 1966080 | tf_op jit(solution)/shard_map/all_to_all | solution.py:490
  24.4 0.1 reshape.65
  24.5 0.5 collective-permute-start.2
  25.1 2.4 %collective-permute-start.1 = (s32[64]{0:T(128)S(1)}, s32[64]{0:T(128)S(1)}, u32[]{:S(2)}, u32[]{:S(2)}) collective-permute-start(s32[64]{0:T(128)S(1)} %reshape.65), channel_id=1, source_target_pairs={{0,64},{32,96},{64,0},{96,32},{1,65},{33,97},{65,1},{97,33},{2,66}... | collective-permute-start | bytes 776 | tf_op jit(solution)/shard_map/ppermute | solution.py:493
  27.5 1.8 %collective-permute-start = (s32[64]{0:T(128)S(1)}, s32[64]{0:T(128)S(1)}, u32[]{:S(2)}, u32[]{:S(2)}) collective-permute-start(s32[64]{0:T(128)S(1)} %reshape.65), channel_id=1, source_target_pairs={{0,32},{32,64},{64,96},{96,0},{1,33},{33,65},{65,97},{97,1},{2,34}... | collective-permute-start | bytes 776 | tf_op jit(solution)/shard_map/ppermute | solution.py:493
  29.3 0.1 concatenate.18
  29.4 0.8 collective-permute-done.1
  30.1 0.9 collective-permute-done
  31.1 0.6 add_subtract_fusion.index_ref
  31.7 4.2 %patch_rows.1 = (f32[64,384]{1,0:T(8,128)}, f32[64,384]{1,0:T(8,128)}, f32[64,384]{1,0:T(8,128)}, f32[64,384]{1,0:T(8,128)}) custom-call(s32[1,256]{1,0:T(1,128)} %add_subtract_fusion.index_ref, f32[192,2048]{1,0:T(8,128)} %bitcast.13, f32[192,2048]{1,0:T(8,128)} %bitcast.14), custom_call_target="tpu_custom_call" | custom-call | tf_op jit(solution)/shard_map/patch_rows/pallas_call | solution.py:453
  35.9 2.3 %collective-permute-start.3 = (f32[64,384]{1,0:T(8,128)}, f32[64,384]{1,0:T(8,128)S(1)}, u32[]{:S(2)}, u32[]{:S(2)}) collective-permute-start(f32[64,384]{1,0:T(8,128)} %get-tuple-element.12), channel_id=1, source_target_pairs={{0,96},{32,0},{64,32},{96,64},{1,97},{33,1},{65,33},{97,65},{2,98}... | collective-permute-start | bytes 294920 | tf_op jit(solution)/shard_map/ppermute | solution.py:499
  38.3 0.9 collective-permute-start.4
  39.2 0.9 collective-permute-start.5
  40.0 0.7 collective-permute-done.3
  40.8 3.8 %collective-permute-done.4 = f32[64,384]{1,0:T(8,128)S(1)} collective-permute-done((f32[64,384]{1,0:T(8,128)}, f32[64,384]{1,0:T(8,128)S(1)}, u32[]{:S(2)}, u32[]{:S(2)}) %collective-permute-start.4) | collective-permute-done | bytes 98336 | tf_op jit(solution)/shard_map/ppermute | solution.py:499
  44.6 0.9 add_add_fusion
  45.5 0.1 reshape.66
  45.7 0.8 reshape.68.wall_ref
  46.4 0.9 copy-done
  47.4 73.2 %near_pairs.1.b_ref = f32[3,8,544]{2,1,0:T(8,128)} custom-call(s32[8]{0:T(128)} %count_ref.1, s32[32]{0:T(128)} %get-tuple-element.15.pick_ref, f32[32,6,2,544]{3,2,1,0:T(2,128)} %copy-done, f32[544,2112]{1,0:T(8,128)} %up_ref.1, f32[3,8,544]{2,1,0:T(8,128)} %bitcast.17, f32[3,8,544]{2,1,0:T(8,128)} %bitcast.20), custom_call_target="tpu_custom_call" | custom-call | tf_op jit(solution)/shard_map/near_pairs/pallas_call | solution.py:360
  120.5 6.4 %wall_pairs.1 = f32[3,8,544]{2,1,0:T(8,128)} custom-call(f32[8,6,512]{2,1,0:T(8,128)} %reshape.68.wall_ref, f32[3,8,544]{2,1,0:T(8,128)} %bitcast.18, f32[3,8,544]{2,1,0:T(8,128)} %near_pairs.1.b_ref), custom_call_target="tpu_custom_call" | custom-call | tf_op jit(solution)/shard_map/wall_pairs/pallas_call | solution.py:345
  (7 shorter events, 0.1 us)
Async XLA Ops:
  0.0 24.4 %copy-start.1 = (s32[8,8]{1,0:T(8,128)S(1)}, s32[8,8]{1,0:T(8,128)}, u32[]{:S(2)}) copy-start(s32[8,8]{1,0:T(8,128)} %param.17) | copy-start | bytes 772
  19.5 26.9 %all-to-all-start.1 = ((f32[32,6,2,544]{3,2,1,0:T(2,128)}), f32[32,6,2,544]{3,2,1,0:T(2,128)S(1)}, u32[]{:S(2)}, u32[]{:S(2)}) async-start(f32[32,6,2,544]{3,2,1,0:T(2,128)} %send_rows.1), calls=%async_computation.1 | async-start | bytes 1966080 | tf_op jit(solution)/shard_map/all_to_all | solution.py:490
  24.5 4.8 %collective-permute-start.2 = (s32[64]{0:T(128)S(1)}, s32[64]{0:T(128)S(1)}, u32[]{:S(2)}, u32[]{:S(2)}) collective-permute-start(s32[64]{0:T(128)S(1)} %reshape.65), channel_id=1, source_target_pairs={{0,96},{32,0},{64,32},{96,64},{1,97},{33,1},{65,33},{97,65},{2,98}... | collective-permute-start | bytes 776 | tf_op jit(solution)/shard_map/ppermute | solution.py:493
  25.1 5.1 %collective-permute-start.1 = (s32[64]{0:T(128)S(1)}, s32[64]{0:T(128)S(1)}, u32[]{:S(2)}, u32[]{:S(2)}) collective-permute-start(s32[64]{0:T(128)S(1)} %reshape.65), channel_id=1, source_target_pairs={{0,64},{32,96},{64,0},{96,32},{1,65},{33,97},{65,1},{97,33},{2,66}... | collective-permute-start | bytes 776 | tf_op jit(solution)/shard_map/ppermute | solution.py:493
  27.5 3.6 %collective-permute-start = (s32[64]{0:T(128)S(1)}, s32[64]{0:T(128)S(1)}, u32[]{:S(2)}, u32[]{:S(2)}) collective-permute-start(s32[64]{0:T(128)S(1)} %reshape.65), channel_id=1, source_target_pairs={{0,32},{32,64},{64,96},{96,0},{1,33},{33,65},{65,97},{97,1},{2,34}... | collective-permute-start | bytes 776 | tf_op jit(solution)/shard_map/ppermute | solution.py:493
  35.9 4.9 %collective-permute-start.3 = (f32[64,384]{1,0:T(8,128)}, f32[64,384]{1,0:T(8,128)S(1)}, u32[]{:S(2)}, u32[]{:S(2)}) collective-permute-start(f32[64,384]{1,0:T(8,128)} %get-tuple-element.12), channel_id=1, source_target_pairs={{0,96},{32,0},{64,32},{96,64},{1,97},{33,1},{65,33},{97,65},{2,98}... | collective-permute-start | bytes 294920 | tf_op jit(solution)/shard_map/ppermute | solution.py:499
  38.3 6.3 %collective-permute-start.4 = (f32[64,384]{1,0:T(8,128)}, f32[64,384]{1,0:T(8,128)S(1)}, u32[]{:S(2)}, u32[]{:S(2)}) collective-permute-start(f32[64,384]{1,0:T(8,128)} %get-tuple-element.13), channel_id=1, source_target_pairs={{0,64},{32,96},{64,0},{96,32},{1,65},{33,97},{65,1},{97,33},{2,66}... | collective-permute-start | bytes 294920 | tf_op jit(solution)/shard_map/ppermute | solution.py:499
  39.2 5.4 %collective-permute-start.5 = (f32[64,384]{1,0:T(8,128)}, f32[64,384]{1,0:T(8,128)S(1)}, u32[]{:S(2)}, u32[]{:S(2)}) collective-permute-start(f32[64,384]{1,0:T(8,128)} %get-tuple-element.14), channel_id=1, source_target_pairs={{0,32},{32,64},{64,96},{96,0},{1,33},{33,65},{65,97},{97,1},{2,34}... | collective-permute-start | bytes 294920 | tf_op jit(solution)/shard_map/ppermute | solution.py:499
  46.4 0.9 copy-start
